TPU v7x, 32 devices: a whole 2x2x4 slice. The times are simulated.
32 devices in a mesh: fsdp: 32 (over z, y, x, core).
Axes of the slice: x: 2, y: 2, z: 4, core: 2. Of those that a mesh axis runs over, the one named last changes fastest.
Arguments:
- inputs: bfloat16 [64, 512, 768], P('fsdp'), may hold values from -6 to 6
- segments: int32 [64, 512], P('fsdp'), may hold values from 0 to 3, never falling along the last dimension, each value on 1 to 256 neighbouring positions
- query_weight: bfloat16 [589824], P('fsdp'), may hold values from -0.21875 to 0.21875
- query_bias: bfloat16 [768], P('fsdp'), may hold values from -3 to 3
- key_weight: bfloat16 [589824], P('fsdp'), may hold values from -0.21875 to 0.21875
- value_weight: bfloat16 [589824], P('fsdp'), may hold values from -0.21875 to 0.21875
- value_bias: bfloat16 [768], P('fsdp'), may hold values from -3 to 3
- output_weight: bfloat16 [589824], P('fsdp'), may hold values from -0.625 to 0.625
- output_bias: bfloat16 [768], P('fsdp'), may hold values from -2 to 2
- attn_gain: bfloat16 [768], P('fsdp'), may hold values from 0.5 to 1.5
- attn_shift: bfloat16 [768], P('fsdp'), may hold values from -2 to 2
- inner_weight: bfloat16 [2359296], P('fsdp'), may hold values from -0.21875 to 0.21875
- inner_bias: bfloat16 [3072], P('fsdp'), may hold values from -3 to 3
- outer_weight: bfloat16 [2359296], P('fsdp'), may hold values from -0.109375 to 0.109375
- outer_bias: bfloat16 [768], P('fsdp'), may hold values from -2 to 2
- ffn_gain: bfloat16 [768], P('fsdp'), may hold values from 0.5 to 1.5
- ffn_shift: bfloat16 [768], P('fsdp'), may hold values from -2 to 2
- cotangent: bfloat16 [64, 512, 768], P('fsdp'), may hold values from -6 to 6
Outputs:
- output: bfloat16 [64, 512, 768], P('fsdp')
- input_grad: bfloat16 [64, 512, 768], P('fsdp')
- query_weight_grad: float32 [589824], P('fsdp')
- query_bias_grad: float32 [768], P('fsdp')
- key_weight_grad: float32 [589824], P('fsdp')
- value_weight_grad: float32 [589824], P('fsdp')
- value_bias_grad: float32 [768], P('fsdp')
- output_weight_grad: float32 [589824], P('fsdp')
- output_bias_grad: float32 [768], P('fsdp')
- attn_gain_grad: float32 [768], P('fsdp')
- attn_shift_grad: float32 [768], P('fsdp')
- inner_weight_grad: float32 [2359296], P('fsdp')
- inner_bias_grad: float32 [3072], P('fsdp')
- outer_weight_grad: float32 [2359296], P('fsdp')
- outer_bias_grad: float32 [768], P('fsdp')
- ffn_gain_grad: float32 [768], P('fsdp')
- ffn_shift_grad: float32 [768], P('fsdp')
Inputs may be any that keep to these rules, and one draw needn't show every extreme that they name: `segments`: within each row of 512 tokens the ids never fall; each of the 4 documents holds 1 to 256 tokens, one exactly 256.
All inputs are finite; a program needn't handle non-finite values.
Results may differ from a plain program's by a relative error of at most 0.013.
Values may be sent and summed in bfloat16 or wider, within the bound.
No kernel may reach another device: no remote copies, remote signals or barrier semaphores. Data moves between devices by JAX's collectives and lax.ppermute only.
A program may use at most 192 MiB of HBM per device.

v0:
```python
import jax
import jax.numpy as jnp
from jax import lax
from jax.sharding import PartitionSpec as P

D = 768
H = 12
HD = 64
FF = 3072


epsilon = 1e-06
masked_score = -1e30
root_half = 0.7071067811865476
inverse_root_twopi = 0.3989422804014327


def matmul(left, right):
    return jnp.dot(left, right, preferred_element_type=jnp.float32)


def matmul_left_t(left, right):
    return lax.dot_general(
        left, right, (((0,), (0,)), ((), ())), preferred_element_type=jnp.float32
    )


def matmul_right_t(left, right):
    return lax.dot_general(
        left, right, (((1,), (1,)), ((), ())), preferred_element_type=jnp.float32
    )


def norm_forward(hidden, gain, shift):
    average = jnp.mean(hidden, axis=-1, keepdims=True)
    centered = hidden - average
    variance = jnp.mean(centered * centered, axis=-1, keepdims=True)
    inv_std = lax.rsqrt(variance + epsilon)
    normed = centered * inv_std
    return (normed * gain + shift, normed, inv_std)


def norm_backward(upstream, normed, inv_std, gain):
    gain_grad = jnp.sum(upstream * normed, axis=0)
    shift_grad = jnp.sum(upstream, axis=0)
    scaled = upstream * gain
    scaled_mean = jnp.mean(scaled, axis=-1, keepdims=True)
    cross_mean = jnp.mean(scaled * normed, axis=-1, keepdims=True)
    return (inv_std * (scaled - scaled_mean - normed * cross_mean), gain_grad, shift_grad)


def gelu_value(inner):
    return 0.5 * inner * (1.0 + lax.erf(inner * root_half))


def gelu_slope(inner):
    return (
        0.5 * (1.0 + lax.erf(inner * root_half))
        + inner * jnp.exp(-0.5 * inner * inner) * inverse_root_twopi
    )


def split_heads(block):
    return block.reshape(block.shape[0], H, HD)


def row_scores(query, key_rows, segment):
    scores = jnp.einsum(
        "qhe,khe->hqk",
        split_heads(query),
        split_heads(key_rows),
        preferred_element_type=jnp.float32,
    ) * HD ** (-0.5)
    same = segment[:, None] == segment[None, :]
    return jnp.where(same[None], scores, masked_score)


def attend_forward(pieces):
    query, key_rows, value_rows, segment = pieces
    scores = row_scores(query, key_rows, segment)
    top = jnp.max(scores, axis=-1, keepdims=True)
    exponent = jnp.exp(scores - top)
    total = jnp.sum(exponent, axis=-1, keepdims=True)
    attention = (exponent / total).astype(jnp.bfloat16)
    context = jnp.einsum(
        "hqk,khe->qhe", attention, split_heads(value_rows), preferred_element_type=jnp.float32
    )
    return (context.reshape(query.shape).astype(jnp.bfloat16), (top + jnp.log(total))[..., 0])


def attend_backward(pieces):
    query, key_rows, value_rows, segment, logsum, context_grad = pieces
    scores = row_scores(query, key_rows, segment)
    attention = jnp.exp(scores - logsum[..., None])
    attention_low = attention.astype(jnp.bfloat16)
    grad_heads = split_heads(context_grad)
    value_grad = jnp.einsum(
        "hqk,qhe->khe", attention_low, grad_heads, preferred_element_type=jnp.float32
    )
    attention_grad = jnp.einsum(
        "qhe,khe->hqk", grad_heads, split_heads(value_rows), preferred_element_type=jnp.float32
    )
    inner_sum = jnp.sum(attention * attention_grad, axis=-1, keepdims=True)
    score_grad = (attention * (attention_grad - inner_sum)).astype(jnp.bfloat16)
    query_grad = jnp.einsum(
        "hqk,khe->qhe", score_grad, split_heads(key_rows), preferred_element_type=jnp.float32
    ) * HD ** (-0.5)
    key_grad = jnp.einsum(
        "hqk,qhe->khe", score_grad, split_heads(query), preferred_element_type=jnp.float32
    ) * HD ** (-0.5)
    shape = query.shape
    return (
        query_grad.reshape(shape).astype(jnp.bfloat16),
        key_grad.reshape(shape).astype(jnp.bfloat16),
        value_grad.reshape(shape).astype(jnp.bfloat16),
    )


def per_device(
    inputs,
    segments,
    query_weight,
    query_bias,
    key_weight,
    value_weight,
    value_bias,
    output_weight,
    output_bias,
    attn_gain,
    attn_shift,
    inner_weight,
    inner_bias,
    outer_weight,
    outer_bias,
    ffn_gain,
    ffn_shift,
    cotangent,
):
    rows, length, width = inputs.shape
    count = rows * length
    attn_parts = (
        query_weight,
        query_bias,
        key_weight,
        value_weight,
        value_bias,
        output_weight,
        output_bias,
        attn_gain,
        attn_shift,
    )
    ffn_parts = (inner_weight, inner_bias, outer_weight, outer_bias, ffn_gain, ffn_shift)
    attn_full = (
        lax.all_gather(query_weight, "fsdp", axis=0, tiled=True),
        lax.all_gather(query_bias, "fsdp", axis=0, tiled=True),
        lax.all_gather(key_weight, "fsdp", axis=0, tiled=True),
        lax.all_gather(value_weight, "fsdp", axis=0, tiled=True),
        lax.all_gather(value_bias, "fsdp", axis=0, tiled=True),
        lax.all_gather(output_weight, "fsdp", axis=0, tiled=True),
        lax.all_gather(output_bias, "fsdp", axis=0, tiled=True),
        lax.all_gather(attn_gain, "fsdp", axis=0, tiled=True),
        lax.all_gather(attn_shift, "fsdp", axis=0, tiled=True),
    )
    ffn_full = (
        lax.all_gather(inner_weight, "fsdp", axis=0, tiled=True),
        lax.all_gather(inner_bias, "fsdp", axis=0, tiled=True),
        lax.all_gather(outer_weight, "fsdp", axis=0, tiled=True),
        lax.all_gather(outer_bias, "fsdp", axis=0, tiled=True),
        lax.all_gather(ffn_gain, "fsdp", axis=0, tiled=True),
        lax.all_gather(ffn_shift, "fsdp", axis=0, tiled=True),
    )

    def shaped(block):
        return block.reshape(rows, length, D)

    flat = inputs.reshape(count, D)
    query = (matmul(flat, attn_full[0].reshape(D, D)) + attn_full[1].astype(jnp.float32)).astype(
        jnp.bfloat16
    )
    key_rows = matmul(flat, attn_full[2].reshape(D, D)).astype(jnp.bfloat16)
    value_rows = (
        matmul(flat, attn_full[3].reshape(D, D)) + attn_full[4].astype(jnp.float32)
    ).astype(jnp.bfloat16)
    context, logsum = lax.map(
        attend_forward, (shaped(query), shaped(key_rows), shaped(value_rows), segments)
    )
    context = context.reshape(count, D)
    attended = matmul(context, attn_full[5].reshape(D, D)) + attn_full[6].astype(jnp.float32)
    first, normed_one, inv_one = norm_forward(
        flat.astype(jnp.float32) + attended,
        attn_full[7].astype(jnp.float32),
        attn_full[8].astype(jnp.float32),
    )
    first_low = first.astype(jnp.bfloat16)
    inner = matmul(first_low, ffn_full[0].reshape(D, FF)) + ffn_full[1].astype(jnp.float32)
    active = gelu_value(inner).astype(jnp.bfloat16)
    outer = matmul(active, ffn_full[2].reshape(FF, D)) + ffn_full[3].astype(jnp.float32)
    result, normed_two, inv_two = norm_forward(
        first + outer, ffn_full[4].astype(jnp.float32), ffn_full[5].astype(jnp.float32)
    )
    ffn_back = (
        lax.all_gather(ffn_parts[0], "fsdp", axis=0, tiled=True),
        lax.all_gather(ffn_parts[1], "fsdp", axis=0, tiled=True),
        lax.all_gather(ffn_parts[2], "fsdp", axis=0, tiled=True),
        lax.all_gather(ffn_parts[3], "fsdp", axis=0, tiled=True),
        lax.all_gather(ffn_parts[4], "fsdp", axis=0, tiled=True),
        lax.all_gather(ffn_parts[5], "fsdp", axis=0, tiled=True),
    )
    upstream = cotangent.reshape(count, D).astype(jnp.float32)
    second_grad, ffn_gain_grad, ffn_shift_grad = norm_backward(
        upstream, normed_two, inv_two, ffn_back[4].astype(jnp.float32)
    )
    outer_grad = second_grad.astype(jnp.bfloat16)
    outer_bias_grad = jnp.sum(outer_grad.astype(jnp.float32), axis=0)
    outer_weight_grad = matmul_left_t(active, outer_grad)
    inner_grad = (
        matmul_right_t(outer_grad, ffn_back[2].reshape(FF, D)) * gelu_slope(inner)
    ).astype(jnp.bfloat16)
    inner_bias_grad = jnp.sum(inner_grad.astype(jnp.float32), axis=0)
    inner_weight_grad = matmul_left_t(first_low, inner_grad)
    first_grad = second_grad + matmul_right_t(inner_grad, ffn_back[0].reshape(D, FF))
    attn_back = (
        lax.all_gather(attn_parts[0], "fsdp", axis=0, tiled=True),
        lax.all_gather(attn_parts[1], "fsdp", axis=0, tiled=True),
        lax.all_gather(attn_parts[2], "fsdp", axis=0, tiled=True),
        lax.all_gather(attn_parts[3], "fsdp", axis=0, tiled=True),
        lax.all_gather(attn_parts[4], "fsdp", axis=0, tiled=True),
        lax.all_gather(attn_parts[5], "fsdp", axis=0, tiled=True),
        lax.all_gather(attn_parts[6], "fsdp", axis=0, tiled=True),
        lax.all_gather(attn_parts[7], "fsdp", axis=0, tiled=True),
        lax.all_gather(attn_parts[8], "fsdp", axis=0, tiled=True),
    )
    attn_pre_grad, attn_gain_grad, attn_shift_grad = norm_backward(
        first_grad, normed_one, inv_one, attn_back[7].astype(jnp.float32)
    )
    attended_grad = attn_pre_grad.astype(jnp.bfloat16)
    output_bias_grad = jnp.sum(attended_grad.astype(jnp.float32), axis=0)
    output_weight_grad = matmul_left_t(context, attended_grad)
    context_grad = matmul_right_t(attended_grad, attn_back[5].reshape(D, D)).astype(jnp.bfloat16)
    query_grad, key_grad, value_grad = lax.map(
        attend_backward,
        (
            shaped(query),
            shaped(key_rows),
            shaped(value_rows),
            segments,
            logsum,
            shaped(context_grad),
        ),
    )
    query_grad = query_grad.reshape(count, D)
    key_grad = key_grad.reshape(count, D)
    value_grad = value_grad.reshape(count, D)
    input_grad = (
        attn_pre_grad
        + matmul_right_t(query_grad, attn_back[0].reshape(D, D))
        + matmul_right_t(key_grad, attn_back[2].reshape(D, D))
        + matmul_right_t(value_grad, attn_back[3].reshape(D, D))
    )
    query_weight_grad = matmul_left_t(flat, query_grad)
    key_weight_grad = matmul_left_t(flat, key_grad)
    value_weight_grad = matmul_left_t(flat, value_grad)
    query_bias_grad = jnp.sum(query_grad.astype(jnp.float32), axis=0)
    value_bias_grad = jnp.sum(value_grad.astype(jnp.float32), axis=0)
    summed = (
        lax.psum_scatter(query_weight_grad.reshape(-1), "fsdp", scatter_dimension=0, tiled=True),
        lax.psum_scatter(query_bias_grad, "fsdp", scatter_dimension=0, tiled=True),
        lax.psum_scatter(key_weight_grad.reshape(-1), "fsdp", scatter_dimension=0, tiled=True),
        lax.psum_scatter(value_weight_grad.reshape(-1), "fsdp", scatter_dimension=0, tiled=True),
        lax.psum_scatter(value_bias_grad, "fsdp", scatter_dimension=0, tiled=True),
        lax.psum_scatter(output_weight_grad.reshape(-1), "fsdp", scatter_dimension=0, tiled=True),
        lax.psum_scatter(output_bias_grad, "fsdp", scatter_dimension=0, tiled=True),
        lax.psum_scatter(attn_gain_grad, "fsdp", scatter_dimension=0, tiled=True),
        lax.psum_scatter(attn_shift_grad, "fsdp", scatter_dimension=0, tiled=True),
        lax.psum_scatter(inner_weight_grad.reshape(-1), "fsdp", scatter_dimension=0, tiled=True),
        lax.psum_scatter(inner_bias_grad, "fsdp", scatter_dimension=0, tiled=True),
        lax.psum_scatter(outer_weight_grad.reshape(-1), "fsdp", scatter_dimension=0, tiled=True),
        lax.psum_scatter(outer_bias_grad, "fsdp", scatter_dimension=0, tiled=True),
        lax.psum_scatter(ffn_gain_grad, "fsdp", scatter_dimension=0, tiled=True),
        lax.psum_scatter(ffn_shift_grad, "fsdp", scatter_dimension=0, tiled=True),
    )
    attn_grads = summed[0:9]
    ffn_grads = summed[9:15]
    return (
        result.reshape(rows, length, D).astype(jnp.bfloat16),
        input_grad.reshape(rows, length, D).astype(jnp.bfloat16),
        attn_grads[0],
        attn_grads[1],
        attn_grads[2],
        attn_grads[3],
        attn_grads[4],
        attn_grads[5],
        attn_grads[6],
        attn_grads[7],
        attn_grads[8],
        ffn_grads[0],
        ffn_grads[1],
        ffn_grads[2],
        ffn_grads[3],
        ffn_grads[4],
        ffn_grads[5],
    )


def solution(mesh):
    return jax.shard_map(
        per_device,
        mesh=mesh,
        in_specs=(
            P("fsdp", None, None),
            P("fsdp", None),
            P("fsdp"),
            P("fsdp"),
            P("fsdp"),
            P("fsdp"),
            P("fsdp"),
            P("fsdp"),
            P("fsdp"),
            P("fsdp"),
            P("fsdp"),
            P("fsdp"),
            P("fsdp"),
            P("fsdp"),
            P("fsdp"),
            P("fsdp"),
            P("fsdp"),
            P("fsdp", None, None),
        ),
        out_specs=(
            P("fsdp", None, None),
            P("fsdp", None, None),
            P("fsdp"),
            P("fsdp"),
            P("fsdp"),
            P("fsdp"),
            P("fsdp"),
            P("fsdp"),
            P("fsdp"),
            P("fsdp"),
            P("fsdp"),
            P("fsdp"),
            P("fsdp"),
            P("fsdp"),
            P("fsdp"),
            P("fsdp"),
            P("fsdp"),
        ),
        check_vma=False,
    )
```

profile of v0, /device:TPU:0, one launch (start us, length us, event | category | flops | bytes accessed | tf_op | source)
XLA Modules:
  0.0 989.8 jit_solution(16271239886015906780)
XLA Ops:
  18.8 42.5 %all-reduce.26 = (bf16[768]{0:T(1024)(128)(2,1)S(1)}, bf16[768]{0:T(1024)(128)(2,1)S(1)}, bf16[768]{0:T(1024)(128)(2,1)S(1)}, bf16[768]{0:T(1024)(128)(2,1)S(1)}...) all-reduce(bf16[768]{0:T(1024)(128)(2,1)S(1)} %dynamic-update-slice, ...), channel_id=1, replica_groups=mesh['fsdp'=32] {'fsdp'}, use_global_device_ids=true, to_apply=%add | all-reduce | flops 9216 | bytes 36864
  63.7 2.7 convert_reduce_fusion.1
  67.9 2.6 reshape.341
  70.4 3.2 add_convert_fusion.2
  75.3 48.6 %all-gather.7.cloned.1.call-done = bf16[589824]{0:T(1024)(128)(2,1)} async-done(((bf16[18432]{0:T(1024)(128)(2,1)}), bf16[589824]{0:T(1024)(128)(2,1)}) %all-gather.7.cloned.1.call-update) | async-done | bytes 1179664 | tf_op jit(solution)/shard_map/all_gather | solution.py:157
  123.9 2.6 reshape.339
  126.4 4.4 add_convert_fusion.3
  130.8 1.7 copy.68
  132.5 47.1 %all-gather.11.cloned.1.call-done = bf16[589824]{0:T(1024)(128)(2,1)} async-done(((bf16[18432]{0:T(1024)(128)(2,1)}), bf16[589824]{0:T(1024)(128)(2,1)}) %all-gather.11.cloned.1.call-update) | async-done | bytes 1179664 | tf_op jit(solution)/shard_map/all_gather | solution.py:156
  179.6 2.6 reshape.343
  182.2 4.4 convolution_convert_fusion.1
  186.6 2.6 copy.70
  189.2 46.0 %all-gather.13.cloned.1.call-done = bf16[589824]{0:T(1024)(128)(2,1)} async-done(((bf16[18432]{0:T(1024)(128)(2,1)}), bf16[589824]{0:T(1024)(128)(2,1)}) %all-gather.13.cloned.1.call-update) | async-done | bytes 1179664 | tf_op jit(solution)/shard_map/all_gather | solution.py:159
  235.2 3.4 reshape.346
  238.6 27.8 %while.26 = (s32[]{:T(128)}, bf16[2,512,768]{2,1,0:T(8,128)(2,1)}, f32[2,12,512]{2,1,0:T(8,128)}, bf16[2,512,768]{1,2,0:T(8,128)(2,1)S(1)}, s32[2,512]{1,0:T(2,1...) while((s32[]{:T(128)}, bf16[2,512,768]{2,1,0:T(8,128)(2,1)}, ...), condition=%wide.region_3.4_spmd, body=%wide.region_0.3_spmd.sunk | while | flops 843704320 | bytes 50018416 | solution.py:184
  240.6 2.1 fusion.107
  242.7 2.6 fusion.108
  245.3 4.4 fusion.109
  254.4 2.1 fusion.107
  256.5 2.6 fusion.108
  259.1 4.4 fusion.109
  266.4 5.3 fusion.39
  271.7 2.4 multiply_reduce_fusion.4
  274.2 26.4 %all-gather.15.cloned.1.call-done = bf16[2359296]{0:T(1024)(128)(2,1)} async-done(((bf16[73728]{0:T(1024)(128)(2,1)}), bf16[2359296]{0:T(1024)(128)(2,1)}) %all-gather.15.cloned.1.call-update) | async-done | bytes 4718608 | tf_op jit(solution)/shard_map/all_gather | solution.py:165
  300.6 8.2 reshape.347
  308.8 12.5 %multiply_convert_fusion.3 = (bf16[1024,3072]{1,0:T(8,128)(2,1)}, f32[1024,3072]{1,0:T(8,128)}) fusion(f32[3072]{0:T(1024)S(1)} %copy-done.37, bf16[768,3072]{1,0:T(8,128)(2,1)} %reshape.347, f32[1024,768]{1,0:T(8,128)} %get-tuple-element.245, f32[768]{0:T(1024)S(1)} %copy-done.30, f32[768]{0:T(1024)S(1)} %copy-done.26, f32[1024]{0:T(1024)S(1)} %add_rsqrt_fusion.1, ...), kind=kOutput, calls=%fused_computation.45 | convolution fusion | flops 4854644736 | bytes 26765312 | tf_op jit(solution)/shard_map/dot_general | solution.py:19
  321.3 44.0 %all-gather.17.cloned.1.call-done = bf16[2359296]{0:T(1024)(128)(2,1)} async-done(((bf16[73728]{0:T(1024)(128)(2,1)}), bf16[2359296]{0:T(1024)(128)(2,1)}) %all-gather.17.cloned.1.call-update) | async-done | bytes 4718608 | tf_op jit(solution)/shard_map/all_gather | solution.py:167
  365.3 9.2 reshape.348
  374.6 9.8 fusion.40
  385.7 1.8 fusion.27
  387.6 2.9 convert_reduce_fusion.2
  390.5 13.7 %convert_reduce_fusion = (f32[3072]{0:T(1024)}, bf16[1024,3072]{1,0:T(8,128)(2,1)S(1)}) fusion(f32[1024,3072]{1,0:T(8,128)} %get-tuple-element.247, f32[3072]{0:T(1024)S(1)} %copy-done.37, bf16[3072,768]{1,0:T(8,128)(2,1)S(1)} %copy-done.12, f32[1024,768]{1,0:T(8,128)S(1)} %get-tuple-element.232), kind=kOutput, calls=%fused_computation.44 | convolution fusion | flops 4873516032 | bytes 26763264 | tf_op jit(solution)/shard_map/dot_general | solution.py:29
  404.2 9.6 multiply_reduce_fusion.1
  413.8 7.6 convolution_bitcast_fusion
  421.5 3.3 convert_reduce_fusion.3
  424.8 2.6 convolution_convert_fusion
  427.4 2.9 fusion.29
  430.8 7.9 fusion.32
  438.7 5.8 copy.90
  444.5 60.9 %while.27 = (s32[]{:T(128)}, bf16[2,512,768]{1,2,0:T(8,128)(2,1)}, bf16[2,512,768]{1,2,0:T(8,128)(2,1)}, bf16[2,512,768]{1,2,0:T(8,128)(2,1)}, bf16[2,512,768]{1...) while((s32[]{:T(128)}, bf16[2,512,768]{1,2,0:T(8,128)(2,1)}, ...), condition=%wide.region_14.15_spmd, body=%wide.region_12.14_spmd.sunk | while | flops 2062673920 | bytes 166377872 | solution.py:240
  449.5 1.8 fusion.120
  451.4 3.2 fusion.121
  454.6 6.8 multiply_reduce_fusion.7
  461.4 7.0 multiply_convert_fusion.7
  468.4 2.0 multiply_convert_fusion.9
  480.0 1.8 fusion.120
  481.8 3.2 fusion.121
  485.0 6.8 multiply_reduce_fusion.7
  491.8 7.0 multiply_convert_fusion.7
  498.8 2.0 multiply_convert_fusion.9
  505.4 4.0 reshape.356
  509.4 2.8 convolution_bitcast_fusion.2
  512.3 2.0 copy.80
  515.9 4.7 convolution_bitcast_fusion.1
  520.6 2.0 copy.81
  524.2 4.7 convolution_bitcast_fusion.3
  528.9 2.0 copy.79
  532.5 10.8 %reshape.358 = f32[2359296]{0:T(1024)} reshape(f32[3072,768]{1,0:T(8,128)} %fusion.32) | data formatting | bytes 18874368 | tf_op jit(solution)/shard_map/reshape | solution.py:277
  543.3 2.7 copy.77
  549.9 41.7 %all-reduce.24 = (f32[768]{0:T(1024)S(1)}, f32[768]{0:T(1024)S(1)}, f32[768]{0:T(1024)S(1)}, f32[768]{0:T(1024)S(1)}, f32[768]{0:T(1024)S(1)}, /*index=5*/f32[30...) all-reduce(f32[768]{0:T(1024)S(1)} %convert_reduce_fusion.5, ...), channel_id=3, replica_groups=mesh['fsdp'=32] {'fsdp'}, use_global_device_ids=true, to_apply=%region_17.18.clone | all-reduce | flops 9216 | bytes 73728
  596.9 3.5 fusion.43
  603.2 2.6 add_convert_fusion
  605.8 367.2 %all-reduce.29.cloned.1.call-done = (f32[589824]{0:T(1024)}, f32[589824]{0:T(1024)}, f32[589824]{0:T(1024)}, f32[589824]{0:T(1024)}, f32[2359296]{0:T(1024)}, /*index=5*/f32[2359296]{0:T(1024)}) async-done(((f32[589824]{0:T(1024)}, f32[589824]{0:T(1024)}, f32[589824]{0:T(1024)}, f32[589824]{0:T(1024)}, f32[2359296]{0:T(1024)}, /*index=5*/f32[2359296]{0:T(1024)}), (f32[589824]{0:T(1024)}, f32[589824]{0:T(1024)}, ...) | async-done | bytes 28311568
  979.1 1.7 dynamic-slice.9
  (229 shorter events, 71.7 us)
Async XLA Ops:
  7.2 60.7 %all-gather.9.cloned.1.call-start = ((), (), s32[]{:S(2)}) async-start(), calls=%async_computation.1 | async-start | bytes 1216512 | tf_op jit(solution)/shard_map/all_gather | solution.py:154
  7.9 115.9 %all-gather.7.cloned.1.call-start = ((), (), s32[]{:S(2)}) async-start(), calls=%async_computation | async-start | bytes 1216512 | tf_op jit(solution)/shard_map/all_gather | solution.py:157
  8.7 170.9 %all-gather.11.cloned.1.call-start = ((), (), s32[]{:S(2)}) async-start(), calls=%async_computation.2 | async-start | bytes 1216512 | tf_op jit(solution)/shard_map/all_gather | solution.py:156
  9.4 225.8 %all-gather.13.cloned.1.call-start = ((), (), s32[]{:S(2)}) async-start(), calls=%async_computation.3 | async-start | bytes 1216512 | tf_op jit(solution)/shard_map/all_gather | solution.py:159
  10.0 290.6 %all-gather.15.cloned.1.call-start = ((), (), s32[]{:S(2)}) async-start(), calls=%async_computation.4 | async-start | bytes 4866048 | tf_op jit(solution)/shard_map/all_gather | solution.py:165
  10.6 354.7 %all-gather.17.cloned.1.call-start = ((), (), s32[]{:S(2)}) async-start(), calls=%async_computation.5 | async-start | bytes 4866048 | tf_op jit(solution)/shard_map/all_gather | solution.py:167
  11.1 961.9 %all-reduce.29.cloned.1.call-start = ((), (), s32[]{:S(2)}) async-start(), calls=%async_computation.6 | async-start | bytes 56623104
  62.5 1.2 copy-start.28
  70.4 3.2 copy-start.22
  126.4 4.4 copy-start.13
  182.2 4.4 copy-start.24
  186.6 52.0 %copy-start.27 = (s32[2,512]{1,0:T(2,128)S(1)}, s32[2,512]{1,0:T(2,128)}, u32[]{:S(2)}) copy-start(s32[2,512]{1,0:T(2,128)} %param.23) | copy-start | bytes 12292
  274.1 34.7 %copy-start.26 = (f32[768]{0:T(1024)S(1)}, f32[768]{0:T(1024)}, u32[]{:S(2)}) copy-start(f32[768]{0:T(1024)} %convert_element_type.178) | copy-start | bytes 9220
  274.1 34.7 %copy-start.30 = (f32[768]{0:T(1024)S(1)}, f32[768]{0:T(1024)}, u32[]{:S(2)}) copy-start(f32[768]{0:T(1024)} %convert_element_type.179) | copy-start | bytes 9220
  274.2 34.7 %copy-start.37 = (f32[3072]{0:T(1024)S(1)}, f32[3072]{0:T(1024)}, u32[]{:S(2)}) copy-start(f32[3072]{0:T(1024)} %convert_element_type.181) | copy-start | bytes 36868
  321.3 53.3 %copy-start.39 = (f32[768]{0:T(1024)S(1)}, f32[768]{0:T(1024)}, u32[]{:S(2)}) copy-start(f32[768]{0:T(1024)} %convert_element_type.183) | copy-start | bytes 9220
  384.3 1.4 copy-start.2
  384.3 1.4 copy-start.29
  384.9 2.7 copy-start.31
  384.9 2.6 copy-start.32
  387.5 2.9 copy-start.12
  387.5 16.6 %slice-start = ((s8[4718592]{0:T(1024)(128)(4,1)}), s8[4194304]{0:T(1024)(128)(4,1)S(1)}, s32[]{:S(2)}) async-start(s8[4718592]{0:T(1024)(128)(4,1)} %bitcast.183), calls=%async_computation.7 | async-start | bytes 8388608
  390.5 13.7 %copy-start.15 = (f32[1024,768]{1,0:T(8,128)}, f32[1024,768]{1,0:T(8,128)S(1)}, u32[]{:S(2)}) copy-start(f32[1024,768]{1,0:T(8,128)S(1)} %get-tuple-element.232) | copy-start | bytes 9437188
  390.5 13.7 %slice-start.1 = ((s8[4718592]{0:T(1024)(128)(4,1)}), s8[524288]{0:T(1024)(128)(4,1)S(1)}, s32[]{:S(2)}) async-start(s8[4718592]{0:T(1024)(128)(4,1)} %bitcast.183), calls=%async_computation.8 | async-start | bytes 1048576
  413.8 7.7 copy-start.17
  421.4 3.3 copy-start.25
  421.5 8.8 slice-start.2
  424.7 2.6 copy-start.3
  424.7 2.6 copy-start.43
  424.8 5.5 slice-start.3
  427.4 3.4 copy-start.16
  444.5 1.1 copy-start
  470.4 1.4 copy-start.8
  470.4 1.9 copy-start.5
  470.4 2.3 copy-start.18
  471.5 3.4 copy-start.1
  472.7 1.1 copy-start.9
  472.9 1.5 copy-start.6
  472.9 2.1 copy-start.19
  475.0 1.1 copy-start
  500.8 1.4 copy-start.8
  500.8 1.9 copy-start.5
  500.9 2.3 copy-start.18
  502.0 3.4 copy-start.1
  503.2 1.1 copy-start.9
  503.4 1.5 copy-start.6
  503.4 2.1 copy-start.19
  505.4 4.0 copy-start.20
  505.4 4.0 copy-start.42
  543.3 2.8 copy-start.7
  543.3 4.3 copy-start.10
  547.6 2.2 copy-start.33
  547.6 2.2 copy-start.34
  547.6 2.2 copy-start.35
  547.7 2.2 copy-start.36
  547.7 2.2 copy-start.38
  547.7 2.2 copy-start.40
  547.7 2.2 copy-start.41
  596.9 3.5 copy-start.21
  596.9 3.5 copy-start.23
  600.4 2.0 copy-start.4
  600.4 2.5 copy-start.11
  600.4 2.8 copy-start.14
Sparse Core Ops, SparseCore 0:
  10.9 56.9 all-gather.8
  70.8 53.0 all-gather.6
  126.8 52.8 all-gather.10
  182.4 52.8 all-gather.12
  238.0 62.5 all-gather.14
  303.4 61.9 all-gather.16
  543.4 429.5 all-reduce.28
where the time goes:
time: 1000 us; the launch traced here: 990 us
  waiting for transfers between devices  583 us (58%)
  matrix products  147 us (15%)
  local copies, waits for them, and re-layouts  122 us (12%)
  blocking collectives  84.2 us (8%)
  other arithmetic  38.4 us (4%)
  between operations  15.2 us (2%)
    unnamed x8, waiting for transfers between devices  371 us
    unnamed x2, blocking collectives  84.2 us
    all_gather x1, waiting for transfers between devices, per_device(): lax.all_gather(value_weight, 'fsdp', axis=0, tiled=True)  48.6 us
    all_gather x1, waiting for transfers between devices, per_device(): lax.all_gather(key_weight, 'fsdp', axis=0, tiled=True)  47.1 us
    all_gather x1, waiting for transfers between devices, per_device(): lax.all_gather(output_weight, 'fsdp', axis=0, tiled=True)  46 us
    all_gather x1, waiting for transfers between devices, per_device(): lax.all_gather(outer_weight, 'fsdp', axis=0, tiled=True)  44 us
    dot_general x6, matrix products, matmul(): return jnp.dot(left, right, preferred_element_type=jnp.float32)  39.6 us
    dot_general x6, matrix products, matmul_right_t(): lax.dot_general(left, right, (((1,), (1,)), ((), ())), preferred_element_...  33.4 us
  transfers between devices with their start and end apart: 7, of which 7 were waited for; matrix products, arithmetic and copies ran while one was open for 12% of the time, Pallas kernels for 0%

commit v1 on v0

v1 whole, which is shorter than its diff:
```python
import jax
import jax.numpy as jnp
from jax import lax
from jax.sharding import PartitionSpec as P

D = 768
H = 12
HD = 64
FF = 3072


epsilon = 1e-06
masked_score = -1e30
root_half = 0.7071067811865476
inverse_root_twopi = 0.3989422804014327


def matmul(left, right):
    return jnp.dot(left, right, preferred_element_type=jnp.float32)


def matmul_left_t(left, right):
    return lax.dot_general(
        left, right, (((0,), (0,)), ((), ())), preferred_element_type=jnp.float32
    )


def matmul_right_t(left, right):
    return lax.dot_general(
        left, right, (((1,), (1,)), ((), ())), preferred_element_type=jnp.float32
    )


def norm_forward(hidden, gain, shift):
    average = jnp.mean(hidden, axis=-1, keepdims=True)
    centered = hidden - average
    variance = jnp.mean(centered * centered, axis=-1, keepdims=True)
    inv_std = lax.rsqrt(variance + epsilon)
    normed = centered * inv_std
    return (normed * gain + shift, normed, inv_std)


def norm_backward(upstream, normed, inv_std, gain):
    gain_grad = jnp.sum(upstream * normed, axis=0)
    shift_grad = jnp.sum(upstream, axis=0)
    scaled = upstream * gain
    scaled_mean = jnp.mean(scaled, axis=-1, keepdims=True)
    cross_mean = jnp.mean(scaled * normed, axis=-1, keepdims=True)
    return (inv_std * (scaled - scaled_mean - normed * cross_mean), gain_grad, shift_grad)


def gelu_value(inner):
    return 0.5 * inner * (1.0 + lax.erf(inner * root_half))


def gelu_slope(inner):
    return (
        0.5 * (1.0 + lax.erf(inner * root_half))
        + inner * jnp.exp(-0.5 * inner * inner) * inverse_root_twopi
    )


def split_heads(block):
    return block.reshape(block.shape[0], H, HD)


def row_scores(query, key_rows, segment):
    scores = jnp.einsum(
        "qhe,khe->hqk",
        split_heads(query),
        split_heads(key_rows),
        preferred_element_type=jnp.float32,
    ) * HD ** (-0.5)
    same = segment[:, None] == segment[None, :]
    return jnp.where(same[None], scores, masked_score)


def attend_forward(pieces):
    query, key_rows, value_rows, segment = pieces
    scores = row_scores(query, key_rows, segment)
    top = jnp.max(scores, axis=-1, keepdims=True)
    exponent = jnp.exp(scores - top)
    total = jnp.sum(exponent, axis=-1, keepdims=True)
    attention = (exponent / total).astype(jnp.bfloat16)
    context = jnp.einsum(
        "hqk,khe->qhe", attention, split_heads(value_rows), preferred_element_type=jnp.float32
    )
    return (context.reshape(query.shape).astype(jnp.bfloat16), (top + jnp.log(total))[..., 0])


def attend_backward(pieces):
    query, key_rows, value_rows, segment, logsum, context_grad = pieces
    scores = row_scores(query, key_rows, segment)
    attention = jnp.exp(scores - logsum[..., None])
    attention_low = attention.astype(jnp.bfloat16)
    grad_heads = split_heads(context_grad)
    value_grad = jnp.einsum(
        "hqk,qhe->khe", attention_low, grad_heads, preferred_element_type=jnp.float32
    )
    attention_grad = jnp.einsum(
        "qhe,khe->hqk", grad_heads, split_heads(value_rows), preferred_element_type=jnp.float32
    )
    inner_sum = jnp.sum(attention * attention_grad, axis=-1, keepdims=True)
    score_grad = (attention * (attention_grad - inner_sum)).astype(jnp.bfloat16)
    query_grad = jnp.einsum(
        "hqk,khe->qhe", score_grad, split_heads(key_rows), preferred_element_type=jnp.float32
    ) * HD ** (-0.5)
    key_grad = jnp.einsum(
        "hqk,qhe->khe", score_grad, split_heads(query), preferred_element_type=jnp.float32
    ) * HD ** (-0.5)
    shape = query.shape
    return (
        query_grad.reshape(shape).astype(jnp.bfloat16),
        key_grad.reshape(shape).astype(jnp.bfloat16),
        value_grad.reshape(shape).astype(jnp.bfloat16),
    )


def per_device(
    inputs,
    segments,
    query_weight,
    query_bias,
    key_weight,
    value_weight,
    value_bias,
    output_weight,
    output_bias,
    attn_gain,
    attn_shift,
    inner_weight,
    inner_bias,
    outer_weight,
    outer_bias,
    ffn_gain,
    ffn_shift,
    cotangent,
):
    rows, length, width = inputs.shape
    count = rows * length
    piece = query_bias.shape[0]
    devices = D // piece
    share = FF // D
    small = jnp.concatenate(
        (
            query_bias,
            value_bias,
            output_bias,
            attn_gain,
            attn_shift,
            outer_bias,
            ffn_gain,
            ffn_shift,
            inner_bias,
        )
    )
    small_rows = jnp.pad(small.reshape(1, -1), ((0, 7), (0, D - small.shape[0])))
    head = jnp.concatenate(
        (
            query_weight.reshape(piece, D),
            key_weight.reshape(piece, D),
            value_weight.reshape(piece, D),
            small_rows,
        )
    )
    inner_local = inner_weight.reshape(piece, FF)
    tail = jnp.concatenate(
        (
            output_weight.reshape(piece, D),
            outer_weight.reshape(share * piece, D),
            inner_local[:, 0:D],
            inner_local[:, D : 2 * D],
            inner_local[:, 2 * D : 3 * D],
            inner_local[:, 3 * D :],
        )
    )
    head_full = lax.all_gather(head, "fsdp", axis=0, tiled=True).reshape(devices, -1, D)
    tail_full = lax.all_gather(tail, "fsdp", axis=0, tiled=True).reshape(devices, -1, D)

    def weight(full, start, size):
        return full[:, start : start + size].reshape(devices * size, D)

    w_query = weight(head_full, 0, piece)
    w_key = weight(head_full, piece, piece)
    w_value = weight(head_full, 2 * piece, piece)
    w_output = weight(tail_full, 0, piece)
    w_outer = weight(tail_full, piece, share * piece)
    w_inner = jnp.concatenate(
        [weight(tail_full, (1 + share + i) * piece, piece) for i in range(share)], axis=1
    )
    small_full = head_full[:, 3 * piece, : (8 + share) * piece].astype(jnp.float32)
    vectors = small_full[:, : 8 * piece].reshape(devices, 8, piece).transpose(1, 0, 2).reshape(8, D)
    b_query, b_value, b_output, gain_one, shift_one, b_outer, gain_two, shift_two = (
        vectors[i] for i in range(8)
    )
    b_inner = small_full[:, 8 * piece :].reshape(FF)

    def shaped(block):
        return block.reshape(rows, length, D)

    flat = inputs.reshape(count, D)
    query = (matmul(flat, w_query) + b_query).astype(jnp.bfloat16)
    key_rows = matmul(flat, w_key).astype(jnp.bfloat16)
    value_rows = (matmul(flat, w_value) + b_value).astype(jnp.bfloat16)
    context, logsum = lax.map(
        attend_forward, (shaped(query), shaped(key_rows), shaped(value_rows), segments)
    )
    context = context.reshape(count, D)
    attended = matmul(context, w_output) + b_output
    first, normed_one, inv_one = norm_forward(
        flat.astype(jnp.float32) + attended, gain_one, shift_one
    )
    first_low = first.astype(jnp.bfloat16)
    inner = matmul(first_low, w_inner) + b_inner
    active = gelu_value(inner).astype(jnp.bfloat16)
    outer = matmul(active, w_outer) + b_outer
    result, normed_two, inv_two = norm_forward(first + outer, gain_two, shift_two)
    upstream = cotangent.reshape(count, D).astype(jnp.float32)
    second_grad, ffn_gain_grad, ffn_shift_grad = norm_backward(
        upstream, normed_two, inv_two, gain_two
    )
    outer_grad = second_grad.astype(jnp.bfloat16)
    outer_bias_grad = jnp.sum(outer_grad.astype(jnp.float32), axis=0)
    outer_weight_grad = matmul_left_t(active, outer_grad)
    inner_grad = (matmul_right_t(outer_grad, w_outer) * gelu_slope(inner)).astype(jnp.bfloat16)
    inner_bias_grad = jnp.sum(inner_grad.astype(jnp.float32), axis=0)
    inner_weight_grads = [
        matmul_left_t(first_low, inner_grad[:, i * D : (i + 1) * D]) for i in range(share)
    ]

    def terms(grad):
        return grad.astype(jnp.bfloat16).reshape(devices, -1, D)

    ffn_terms = jnp.concatenate(
        [terms(outer_weight_grad)] + [terms(block) for block in inner_weight_grads], axis=1
    )
    ffn_sum = lax.psum_scatter(
        ffn_terms.reshape(-1, D), "fsdp", scatter_dimension=0, tiled=True
    ).astype(jnp.float32)
    first_grad = second_grad + matmul_right_t(inner_grad, w_inner)
    attn_pre_grad, attn_gain_grad, attn_shift_grad = norm_backward(
        first_grad, normed_one, inv_one, gain_one
    )
    attended_grad = attn_pre_grad.astype(jnp.bfloat16)
    output_bias_grad = jnp.sum(attended_grad.astype(jnp.float32), axis=0)
    output_weight_grad = matmul_left_t(context, attended_grad)
    context_grad = matmul_right_t(attended_grad, w_output).astype(jnp.bfloat16)
    query_grad, key_grad, value_grad = lax.map(
        attend_backward,
        (
            shaped(query),
            shaped(key_rows),
            shaped(value_rows),
            segments,
            logsum,
            shaped(context_grad),
        ),
    )
    query_grad = query_grad.reshape(count, D)
    key_grad = key_grad.reshape(count, D)
    value_grad = value_grad.reshape(count, D)
    query_weight_grad = matmul_left_t(flat, query_grad)
    key_weight_grad = matmul_left_t(flat, key_grad)
    value_weight_grad = matmul_left_t(flat, value_grad)
    query_bias_grad = jnp.sum(query_grad.astype(jnp.float32), axis=0)
    value_bias_grad = jnp.sum(value_grad.astype(jnp.float32), axis=0)
    small_terms = jnp.stack(
        (
            query_bias_grad,
            value_bias_grad,
            output_bias_grad,
            attn_gain_grad,
            attn_shift_grad,
            outer_bias_grad,
            ffn_gain_grad,
            ffn_shift_grad,
        )
    )
    small_terms = jnp.concatenate(
        (
            small_terms.reshape(8, devices, piece).transpose(1, 0, 2).reshape(devices, 8 * piece),
            inner_bias_grad.reshape(devices, share * piece),
        ),
        axis=1,
    ).astype(jnp.bfloat16)
    small_terms = jnp.pad(
        small_terms[:, None, :], ((0, 0), (0, 7), (0, D - small_terms.shape[1]))
    )
    attn_terms = jnp.concatenate(
        (
            terms(output_weight_grad),
            terms(query_weight_grad),
            terms(key_weight_grad),
            terms(value_weight_grad),
            small_terms,
        ),
        axis=1,
    )
    attn_sum = lax.psum_scatter(
        attn_terms.reshape(-1, D), "fsdp", scatter_dimension=0, tiled=True
    ).astype(jnp.float32)
    input_grad = (
        attn_pre_grad
        + matmul_right_t(query_grad, w_query)
        + matmul_right_t(key_grad, w_key)
        + matmul_right_t(value_grad, w_value)
    )

    def owned(total, start, size):
        return total[start : start + size].reshape(-1)

    small_sum = attn_sum[4 * piece, : (8 + share) * piece]

    def vector(i, size=1):
        return small_sum[i * piece : (i + size) * piece]

    inner_sum = jnp.concatenate(
        [ffn_sum[(share + i) * piece : (share + i + 1) * piece] for i in range(share)], axis=1
    )
    return (
        result.reshape(rows, length, D).astype(jnp.bfloat16),
        input_grad.reshape(rows, length, D).astype(jnp.bfloat16),
        owned(attn_sum, piece, piece),
        vector(0),
        owned(attn_sum, 2 * piece, piece),
        owned(attn_sum, 3 * piece, piece),
        vector(1),
        owned(attn_sum, 0, piece),
        vector(2),
        vector(3),
        vector(4),
        inner_sum.reshape(-1),
        vector(8, share),
        owned(ffn_sum, 0, share * piece),
        vector(5),
        vector(6),
        vector(7),
    )


def solution(mesh):
    return jax.shard_map(
        per_device,
        mesh=mesh,
        in_specs=(
            P("fsdp", None, None),
            P("fsdp", None),
            P("fsdp"),
            P("fsdp"),
            P("fsdp"),
            P("fsdp"),
            P("fsdp"),
            P("fsdp"),
            P("fsdp"),
            P("fsdp"),
            P("fsdp"),
            P("fsdp"),
            P("fsdp"),
            P("fsdp"),
            P("fsdp"),
            P("fsdp"),
            P("fsdp"),
            P("fsdp", None, None),
        ),
        out_specs=(
            P("fsdp", None, None),
            P("fsdp", None, None),
            P("fsdp"),
            P("fsdp"),
            P("fsdp"),
            P("fsdp"),
            P("fsdp"),
            P("fsdp"),
            P("fsdp"),
            P("fsdp"),
            P("fsdp"),
            P("fsdp"),
            P("fsdp"),
            P("fsdp"),
            P("fsdp"),
            P("fsdp"),
            P("fsdp"),
        ),
        check_vma=False,
    )
```

time: 1000 us -> 602 us (0.60)
  waiting for transfers between devices: 583 us -> 311 us
  blocking collectives: 84.2 us -> 0 us
  local copies, waits for them, and re-layouts: 122 us -> 84.4 us
    unnamed x8 -> x4, waiting for transfers between devices: 371 us -> 0.07 us
    reduce_scatter x0 -> x2, waiting for transfers between devices: none -> 206 us  [the longest x1 135 us: per_device(): lax.psum_scatter(ffn_terms.reshape(-1, D), 'fsdp', scatter_dimension=0, t...]
    all_gather x6 -> x2, waiting for transfers between devices: 212 us -> 105 us  [the longest x1 58.9 us: per_device(): lax.all_gather(head, 'fsdp', axis=0, tiled=True).reshape(devices, -1, D)]
    unnamed x2 -> x0, blocking collectives: 84.2 us -> none
    reshape x11 -> x14, local copies, waits for them, and re-layouts: 48 us -> 8.94 us  [the longest x5 3.28 us: owned(): return total[start:start + size].reshape(-1)]
    dot_general x6, matrix products: 39.6 us -> 24.4 us  [matmul(): return jnp.dot(left, right, preferred_element_type=jnp.float32)]
    slice x0 -> x11, local copies, waits for them, and re-layouts: none -> 13.8 us  [the longest x3 9.59 us: weight(): return full[:, start:start + size].reshape(devices * size, D)]
    unnamed x115 -> x114, local copies, waits for them, and re-layouts: 31.6 us -> 19.5 us
  transfers between devices with their start and end apart: 7 -> 4, of which waited for: 7 -> 4; matrix products, arithmetic and copies ran while one was open for 12% -> 15% of each run, Pallas kernels for 0% -> 0%
where the time goes in v1:
time: 602 us; the launch traced here: 595 us
  waiting for transfers between devices  311 us (52%)
  matrix products  148 us (25%)
  local copies, waits for them, and re-layouts  84.4 us (14%)
  other arithmetic  36.4 us (6%)
  between operations  15.1 us (3%)
    reduce_scatter x1, waiting for transfers between devices, per_device(): lax.psum_scatter(ffn_terms.reshape(-1, D), 'fsdp', scatter_dimension=0, t...  135 us
    reduce_scatter x1, waiting for transfers between devices, per_device(): lax.psum_scatter(attn_terms.reshape(-1, D), 'fsdp', scatter_dimension=0,...  70.5 us
    all_gather x1, waiting for transfers between devices, per_device(): lax.all_gather(head, 'fsdp', axis=0, tiled=True).reshape(devices, -1, D)  58.9 us
    all_gather x1, waiting for transfers between devices, per_device(): lax.all_gather(tail, 'fsdp', axis=0, tiled=True).reshape(devices, -1, D)  45.8 us
    dot_general x6, matrix products, matmul_right_t(): lax.dot_general(left, right, (((1,), (1,)), ((), ())), preferred_element_...  34.5 us
    dot_general x9, matrix products, matmul_left_t(): lax.dot_general(left, right, (((0,), (0,)), ((), ())), preferred_element_...  30.4 us
    dot_general x6, matrix products, matmul(): return jnp.dot(left, right, preferred_element_type=jnp.float32)  24.4 us
    dot_general x2, matrix products, attend_backward(): jnp.einsum('qhe,khe->hqk', grad_heads, split_heads(value_rows), preferred...  21.9 us
  transfers between devices with their start and end apart: 4, of which 4 were waited for; matrix products, arithmetic and copies ran while one was open for 15% of the time, Pallas kernels for 0%

profile of v1, /device:TPU:0, one launch (start us, length us, event | category | flops | bytes accessed | tf_op | source)
XLA Modules:
  0.0 595.0 jit_solution(14103868544412942767)
XLA Ops:
  9.8 6.1 %concatenate.38 = bf16[288]{0:T(512)(128)(2,1)S(1)} concatenate(bf16[24]{0:T(256)(128)(2,1)} %param.25, bf16[24]{0:T(256)(128)(2,1)} %param.28, bf16[24]{0:T(256)(128)(2,1)} %param.30, bf16[24]{0:T(256)(128)(2,1)} %param.31, bf16[24]{0:T(256)(128)(2,1)} %param.32, bf16[24]{0:T(256)(128)(2,1)} %param.36, bf16[24]{0:T(256)(128)(2,1)} %param.37, bf16[24]{0:T(256)(128)(2,1)} %param.38, ...), dimensions={0} | concatenate | bytes 1152 | tf_op jit(solution)/shard_map/concatenate | solution.py:144
  21.5 58.9 %all-gather.3.cloned.1.call-done = bf16[2560,768]{1,0:T(8,128)(2,1)} async-done(((bf16[80,768]{1,0:T(8,128)(2,1)}), bf16[2560,768]{1,0:T(8,128)(2,1)}) %all-gather.3.cloned.1.call-update) | async-done | bytes 3932176 | tf_op jit(solution)/shard_map/all_gather | solution.py:177
  82.1 3.4 fusion.60
  85.5 1.5 add_convert_fusion.3
  90.7 1.8 fusion.26
  93.1 3.0 convolution_convert_fusion.2
  96.1 1.5 add_convert_fusion.2
  97.7 1.9 copy_bitcast_fusion
  99.6 24.1 %while.26 = (s32[]{:T(128)}, bf16[2,512,768]{2,1,0:T(8,128)(2,1)}, f32[2,12,512]{2,1,0:T(8,128)}, bf16[2,512,768]{1,2,0:T(8,128)(2,1)S(1)}, s32[2,512]{1,0:T(2,1...) while((s32[]{:T(128)}, bf16[2,512,768]{2,1,0:T(8,128)(2,1)}, ...), condition=%wide.region_3.4_spmd, body=%wide.region_0.3_spmd.sunk | while | flops 843704320 | bytes 50019424 | solution.py:205
  99.8 1.5 constant_dynamic-slice_fusion.19
  101.5 2.1 fusion.134
  103.6 2.6 fusion.135
  106.9 3.6 fusion.136
  111.7 1.5 constant_dynamic-slice_fusion.19
  113.4 2.1 fusion.134
  115.5 2.6 fusion.135
  118.8 3.6 fusion.136
  123.6 45.8 %all-gather.5.cloned.1.call-done = bf16[6912,768]{1,0:T(8,128)(2,1)} async-done(((bf16[216,768]{1,0:T(8,128)(2,1)}), bf16[6912,768]{1,0:T(8,128)(2,1)}) %all-gather.5.cloned.1.call-update) | async-done | bytes 10616848 | tf_op jit(solution)/shard_map/all_gather | solution.py:178
  169.4 3.1 fusion.59
  172.5 3.1 slice.258
  176.2 1.6 fusion.63
  179.1 11.4 %multiply_convert_fusion.3 = (bf16[1024,3072]{1,0:T(8,128)(2,1)S(1)}, f32[1024,3072]{1,0:T(8,128)}) fusion(f32[3072]{0:T(1024)S(1)} %copy-done.34, bf16[1024,768]{1,0:T(8,128)(2,1)S(1)} %fusion.28, bf16[768,768]{1,0:T(8,128)(2,1)S(1)} %bitcast.262, bf16[768,768]{1,0:T(8,128)(2,1)S(1)} %bitcast.264, bf16[768,768]{1,0:T(8,128)(2,1)S(1)} %bitcast.266, ...), kind=kOutput, calls=%fused_computation.44 | convolution fusion | flops 4869586944 | bytes 25178112 | tf_op jit(solution)/shard_map/dot_general | solution.py:19
  190.5 2.7 copy-done.47
  193.2 5.5 fusion.64
  200.1 3.3 fusion.27
  203.4 1.8 convert_reduce_fusion.1
  205.2 14.9 %fusion.65 = (bf16[3072]{0:T(1024)(128)(2,1)}, bf16[1024,3072]{1,0:T(8,128)(2,1)}) fusion(f32[1024,3072]{1,0:T(8,128)} %get-tuple-element.253, f32[3072]{0:T(1024)S(1)} %copy-done.34, bf16[3072,768]{1,0:T(8,128)(2,1)S(1)} %bitcast.245, f32[1024,768]{1,0:T(8,128)S(1)} %get-tuple-element.214), kind=kOutput, calls=%fused_computation.167 | convolution fusion | flops 4870370304 | bytes 26757120 | tf_op jit(solution)/shard_map/dot_general | solution.py:29
  220.1 9.5 %multiply_reduce_fusion.1 = (bf16[768]{0:T(1024)(128)(2,1)}, f32[1024]{0:T(1024)S(1)}, f32[1024]{0:T(1024)S(1)}, bf16[768]{0:T(1024)(128)(2,1)}, f32[1024,768]{1,0:T(8,128)S(1)}) fusion(f32[1024,768]{1,0:T(8,128)S(1)} %get-tuple-element.251, f32[1024]{0:T(1024)S(1)} %add_rsqrt_fusion.1, f32[1024]{0:T(1024)S(1)} %broadcast_multiply_fusion.4, ...), kind=kOutput, calls=%fused_computation.58 | convolution fusion | flops 4858572800 | bytes 20469760 | tf_op jit(solution)/shard_map/dot_general | solution.py:29
  229.6 1.8 convert_reduce_fusion
  231.4 2.6 convolution_convert_fusion.1
  234.1 2.5 convolution_convert_fusion.3
  236.6 77.9 %while.27 = (s32[]{:T(128)}, bf16[2,512,768]{1,2,0:T(8,128)(2,1)}, bf16[2,512,768]{1,2,0:T(8,128)(2,1)}, bf16[2,512,768]{1,2,0:T(8,128)(2,1)}, bf16[2,512,768]{1...) while((s32[]{:T(128)}, bf16[2,512,768]{1,2,0:T(8,128)(2,1)}, ...), condition=%wide.region_14.15_spmd, body=%wide.region_12.14_spmd.sunk | while | flops 2062673920 | bytes 185253232 | solution.py:248
  236.6 1.7 constant_dynamic-slice_fusion.20
  239.5 6.4 %fusion.147 = f32[12,512,512]{1,2,0:T(8,128)} fusion(bf16[512,12,64]{0,2,1:T(8,128)(2,1)S(1)} %bitcast.227, bf16[512,12,64]{0,2,1:T(8,128)(2,1)S(1)} %bitcast.225), kind=kOutput, calls=%fused_computation.168.clone.1 | convolution fusion | flops 402653184 | bytes 14155776 | tf_op jit(solution)/shard_map/while/body/eval_jaxpr/qhe,khe->hqk/dot_general | solution.py:68
  247.7 11.0 %multiply_reduce_fusion.7 = (f32[12,512]{1,0:T(8,128)S(1)}, f32[12,512,512]{1,2,0:T(8,128)}) fusion(f32[12,512,512]{1,2,0:T(8,128)} %fusion.147, f32[12,512]{1,0:T(8,128)S(1)} %dynamic-slice_bitcast_fusion.2, pred[512,512]{0,1:T(8,128)(4,1)S(1)} %broadcast_compare_fusion.5, bf16[512,12,64]{0,2,1:T(8,128)(2,1)S(1)} %bitcast.230, ...), kind=kOutput, calls=%fused_computation.17.clone.1 | convolution fusion | flops 418375680 | bytes 27049984 | tf_op jit(solution)/shard_map/while/body/eval_jaxpr/qhe,khe->hqk/dot_general | solution.py:100
  258.7 1.6 slice-done.2
  260.4 6.9 %multiply_convert_fusion.7 = bf16[12,512,512]{1,2,0:T(8,128)(2,1)S(1)} fusion(f32[12,512,512]{1,2,0:T(8,128)} %get-tuple-element.377, f32[12,512,512]{1,2,0:T(8,128)S(1)} %bitcast.224, f32[12,512]{1,0:T(8,128)S(1)} %get-tuple-element.378, f32[12,512]{1,0:T(8,128)S(1)} %dynamic-slice_bitcast_fusion.2, pred[512,512]{0,1:T(8,128)(4,1)S(1)} %broadcast_compare_fusion.5), kind=kLoop, calls=%fused_computation.16.clone.1 | loop fusion | flops 18874368 | bytes 31768576 | tf_op jit(solution)/shard_map/while/body/eval_jaxpr/convert_element_type | solution.py:104
  267.3 2.0 multiply_convert_fusion.9
  269.3 3.1 fusion.148
  275.5 1.7 constant_dynamic-slice_fusion.20
  278.4 6.4 %fusion.147 = f32[12,512,512]{1,2,0:T(8,128)} fusion(bf16[512,12,64]{0,2,1:T(8,128)(2,1)S(1)} %bitcast.227, bf16[512,12,64]{0,2,1:T(8,128)(2,1)S(1)} %bitcast.225), kind=kOutput, calls=%fused_computation.168.clone.1 | convolution fusion | flops 402653184 | bytes 14155776 | tf_op jit(solution)/shard_map/while/body/eval_jaxpr/qhe,khe->hqk/dot_general | solution.py:68
  286.7 11.0 %multiply_reduce_fusion.7 = (f32[12,512]{1,0:T(8,128)S(1)}, f32[12,512,512]{1,2,0:T(8,128)}) fusion(f32[12,512,512]{1,2,0:T(8,128)} %fusion.147, f32[12,512]{1,0:T(8,128)S(1)} %dynamic-slice_bitcast_fusion.2, pred[512,512]{0,1:T(8,128)(4,1)S(1)} %broadcast_compare_fusion.5, bf16[512,12,64]{0,2,1:T(8,128)(2,1)S(1)} %bitcast.230, ...), kind=kOutput, calls=%fused_computation.17.clone.1 | convolution fusion | flops 418375680 | bytes 27049984 | tf_op jit(solution)/shard_map/while/body/eval_jaxpr/qhe,khe->hqk/dot_general | solution.py:100
  297.6 1.6 slice-done.2
  299.3 6.9 %multiply_convert_fusion.7 = bf16[12,512,512]{1,2,0:T(8,128)(2,1)S(1)} fusion(f32[12,512,512]{1,2,0:T(8,128)} %get-tuple-element.377, f32[12,512,512]{1,2,0:T(8,128)S(1)} %bitcast.224, f32[12,512]{1,0:T(8,128)S(1)} %get-tuple-element.378, f32[12,512]{1,0:T(8,128)S(1)} %dynamic-slice_bitcast_fusion.2, pred[512,512]{0,1:T(8,128)(4,1)S(1)} %broadcast_compare_fusion.5), kind=kLoop, calls=%fused_computation.16.clone.1 | loop fusion | flops 18874368 | bytes 31768576 | tf_op jit(solution)/shard_map/while/body/eval_jaxpr/convert_element_type | solution.py:104
  306.2 2.0 multiply_convert_fusion.9
  308.2 3.0 fusion.148
  314.4 1.7 reduce.4
  316.1 4.5 bitcast_convert_fusion.2
  320.9 4.0 bitcast_convert_fusion
  326.1 2.4 constant_dynamic-update-slice_fusion.21
  328.5 2.9 bitcast_convert_fusion.1
  335.8 8.4 %convolution_convert_fusion = bf16[3072,768]{1,0:T(8,128)(2,1)S(1)} fusion(bf16[1024,3072]{1,0:T(8,128)(2,1)} %copy-done.47, f32[1024,768]{1,0:T(8,128)} %copy-done.12), kind=kOutput, calls=%fused_computation.46 | convolution fusion | flops 4834983936 | bytes 14155776 | tf_op jit(solution)/shard_map/dot_general | solution.py:23
  344.3 2.7 constant_dynamic-update-slice_fusion.26
  347.1 3.7 fusion.37
  352.0 1.5 fusion.40
  354.6 1.5 fusion.43
  357.2 1.5 fusion.46
  359.8 2.7 copy.87
  362.4 1.6 copy.88
  365.0 3.4 fusion.67
  368.4 1.4 fusion.68
  370.7 2.7 add_convert_fusion
  373.4 70.5 %reduce-scatter.3.cloned.1.call-done = bf16[104,768]{1,0:T(8,128)(2,1)} async-done(((bf16[3328,768]{1,0:T(8,128)(2,1)}), bf16[104,768]{1,0:T(8,128)(2,1)}) %reduce-scatter.3.cloned.1.call-update) | async-done | bytes 159760 | tf_op jit(solution)/shard_map/reduce_scatter | solution.py:299
  449.5 135.3 %reduce-scatter.5.cloned.1.call-done = bf16[192,768]{1,0:T(8,128)(2,1)} async-done(((bf16[6144,768]{1,0:T(8,128)(2,1)}), bf16[192,768]{1,0:T(8,128)(2,1)}) %reduce-scatter.5.cloned.1.call-update) | async-done | bytes 294928 | tf_op jit(solution)/shard_map/reduce_scatter | solution.py:237
  (254 shorter events, 54.6 us)
Async XLA Ops:
  7.2 13.3 %copy-start.2 = (bf16[2,512,768]{2,1,0:T(8,128)(2,1)S(1)}, bf16[2,512,768]{2,1,0:T(8,128)(2,1)}, u32[]{:S(2)}) copy-start(bf16[2,512,768]{2,1,0:T(8,128)(2,1)} %param.39) | copy-start | bytes 4718596
  7.2 73.1 %all-gather.3.cloned.1.call-start = ((), (), s32[]{:S(2)}) async-start(), calls=%async_computation.2 | async-start | bytes 4055040 | tf_op jit(solution)/shard_map/all_gather | solution.py:177
  16.6 152.7 %all-gather.5.cloned.1.call-start = ((), (), s32[]{:S(2)}) async-start(), calls=%async_computation.3 | async-start | bytes 10948608 | tf_op jit(solution)/shard_map/all_gather | solution.py:178
  19.6 0.7 copy-start.25
  20.4 423.5 %reduce-scatter.3.cloned.1.call-start = ((), (), s32[]{:S(2)}) async-start(), calls=%async_computation.4 | async-start | bytes 5271552 | tf_op jit(solution)/shard_map/reduce_scatter | solution.py:299
  82.0 3.4 copy-start.42
  85.5 1.5 copy-start.10
  85.5 7.7 %copy-start.19 = (bf16[32,24,768]{2,1,0:T(8,128)(2,1)}, bf16[32,24,768]{2,1,0:T(8,128)(2,1)S(1)}, u32[]{:S(2)}) copy-start(bf16[32,24,768]{2,1,0:T(8,128)(2,1)S(1)} %get-tuple-element.230) | copy-start | bytes 3538948
  90.0 6.1 %copy-start.27 = (f32[768]{0:T(1024)}, f32[768]{0:T(1024)S(1)}, u32[]{:S(2)}) copy-start(f32[768]{0:T(1024)S(1)} %mul.165) | copy-start | bytes 9220
  93.1 3.0 copy-start.21
  93.1 3.0 copy-start.43
  97.6 1.9 copy-start.26
  172.5 6.6 %copy-start.17 = (bf16[32,24,768]{2,1,0:T(8,128)(2,1)}, bf16[32,24,768]{2,1,0:T(8,128)(2,1)S(1)}, u32[]{:S(2)}) copy-start(bf16[32,24,768]{2,1,0:T(8,128)(2,1)S(1)} %get-tuple-element.228) | copy-start | bytes 3538948
  172.5 3.3 copy-start.44
  172.5 3.7 copy-start.45
  177.8 0.7 copy-start.32
  178.3 0.7 copy-start.34
  179.1 11.5 %copy-start.15 = (bf16[1024,768]{1,0:T(8,128)(2,1)}, bf16[1024,768]{1,0:T(8,128)(2,1)S(1)}, u32[]{:S(2)}) copy-start(bf16[1024,768]{1,0:T(8,128)(2,1)S(1)} %fusion.28) | copy-start | bytes 4718596
  179.1 14.1 %copy-start.39 = (f32[768]{0:T(1024)S(1)}, f32[768]{0:T(1024)}, u32[]{:S(2)}) copy-start(f32[768]{0:T(1024)} %add.160) | copy-start | bytes 9220
  190.5 2.7 copy-start.47
  198.7 1.4 copy-start.3
  198.7 1.4 copy-start.28
  198.7 1.4 copy-start.31
  200.1 3.3 copy-start.33
  205.2 14.9 %copy-start.12 = (f32[1024,768]{1,0:T(8,128)}, f32[1024,768]{1,0:T(8,128)S(1)}, u32[]{:S(2)}) copy-start(f32[1024,768]{1,0:T(8,128)S(1)} %get-tuple-element.214) | copy-start | bytes 9437188
  205.2 14.9 %copy-start.18 = (bf16[32,24,768]{2,1,0:T(8,128)(2,1)S(1)}, bf16[32,24,768]{2,1,0:T(8,128)(2,1)}, u32[]{:S(2)}) copy-start(bf16[32,24,768]{2,1,0:T(8,128)(2,1)} %copy-done.17) | copy-start | bytes 3538948
  231.4 2.6 copy-start.4
  231.4 2.6 copy-start.46
  234.1 2.5 copy-start.24
  236.6 1.7 copy-start
  239.5 6.7 %copy-start.6 = (bf16[2,512,768]{2,1,0:T(8,128)(2,1)S(1)}, bf16[2,512,768]{2,1,0:T(8,128)(2,1)}, u32[]{:S(2)}) copy-start(bf16[2,512,768]{2,1,0:T(8,128)(2,1)} %get-tuple-element.435) | copy-start | bytes 4718596 | tf_op jit(solution)/shard_map/while
  247.7 11.0 %slice-start = ((s8[12582912]{0:T(1024)(128)(4,1)}), s8[4194304]{0:T(1024)(128)(4,1)S(1)}, s32[]{:S(2)}) async-start(s8[12582912]{0:T(1024)(128)(4,1)} %bitcast.223), calls=%async_computation.6 | async-start | bytes 8388608 | tf_op jit(solution)/shard_map/while
  247.7 11.0 %slice-start.1 = ((s8[12582912]{0:T(1024)(128)(4,1)}), s8[4194304]{0:T(1024)(128)(4,1)S(1)}, s32[]{:S(2)}) async-start(s8[12582912]{0:T(1024)(128)(4,1)} %bitcast.223), calls=%async_computation.7 | async-start | bytes 8388608 | tf_op jit(solution)/shard_map/while
  247.7 12.6 %slice-start.2 = ((s8[12582912]{0:T(1024)(128)(4,1)}), s8[4194304]{0:T(1024)(128)(4,1)S(1)}, s32[]{:S(2)}) async-start(s8[12582912]{0:T(1024)(128)(4,1)} %bitcast.223), calls=%async_computation.8 | async-start | bytes 8388608 | tf_op jit(solution)/shard_map/while
  269.3 3.1 copy-start.7
  273.4 1.1 copy-start.8
  273.4 2.1 copy-start.1
  275.5 1.7 copy-start
  278.4 6.7 %copy-start.6 = (bf16[2,512,768]{2,1,0:T(8,128)(2,1)S(1)}, bf16[2,512,768]{2,1,0:T(8,128)(2,1)}, u32[]{:S(2)}) copy-start(bf16[2,512,768]{2,1,0:T(8,128)(2,1)} %get-tuple-element.435) | copy-start | bytes 4718596 | tf_op jit(solution)/shard_map/while
  286.6 11.0 %slice-start = ((s8[12582912]{0:T(1024)(128)(4,1)}), s8[4194304]{0:T(1024)(128)(4,1)S(1)}, s32[]{:S(2)}) async-start(s8[12582912]{0:T(1024)(128)(4,1)} %bitcast.223), calls=%async_computation.6 | async-start | bytes 8388608 | tf_op jit(solution)/shard_map/while
  286.6 11.0 %slice-start.1 = ((s8[12582912]{0:T(1024)(128)(4,1)}), s8[4194304]{0:T(1024)(128)(4,1)S(1)}, s32[]{:S(2)}) async-start(s8[12582912]{0:T(1024)(128)(4,1)} %bitcast.223), calls=%async_computation.7 | async-start | bytes 8388608 | tf_op jit(solution)/shard_map/while
  286.7 12.6 %slice-start.2 = ((s8[12582912]{0:T(1024)(128)(4,1)}), s8[4194304]{0:T(1024)(128)(4,1)S(1)}, s32[]{:S(2)}) async-start(s8[12582912]{0:T(1024)(128)(4,1)} %bitcast.223), calls=%async_computation.8 | async-start | bytes 8388608 | tf_op jit(solution)/shard_map/while
  308.2 3.1 copy-start.7
  312.3 1.1 copy-start.8
  312.3 2.1 copy-start.1
  316.1 4.5 copy-start.9
  320.9 4.3 copy-start.36
  320.9 4.4 copy-start.41
  320.9 4.5 copy-start.40
  320.9 4.6 copy-start.37
  320.9 4.7 copy-start.35
  320.9 4.8 copy-start.30
  320.9 5.0 copy-start.38
  320.9 7.6 %copy-start.13 = (bf16[2,512,768]{1,2,0:T(8,128)(2,1)S(1)}, bf16[2,512,768]{1,2,0:T(8,128)(2,1)}, u32[]{:S(2)}) copy-start(bf16[2,512,768]{1,2,0:T(8,128)(2,1)} %get-tuple-element.112) | copy-start | bytes 4718596
  328.5 3.0 copy-start.23
  331.5 2.3 copy-start.22
  335.8 249.0 %reduce-scatter.5.cloned.1.call-start = ((), (), s32[]{:S(2)}) async-start(), calls=%async_computation.5 | async-start | bytes 9732096 | tf_op jit(solution)/shard_map/reduce_scatter | solution.py:237
  344.3 2.8 copy-start.16
  344.3 7.7 %slice-start.3 = ((s8[6291456]{0:T(1024)(128)(4,1)}), s8[4194304]{0:T(1024)(128)(4,1)S(1)}, s32[]{:S(2)}) async-start(s8[6291456]{0:T(1024)(128)(4,1)} %bitcast.294), calls=%async_computation.9 | async-start | bytes 8388608
  347.1 4.9 slice-start.4
  365.0 3.4 copy-start.14
  365.0 3.4 copy-start.20
  368.4 2.0 copy-start.5
  368.4 2.3 copy-start.11
  (1 other events, 0.7 us)
Sparse Core Ops, SparseCore 0:
  16.8 63.5 all-gather.2
  83.8 85.5 all-gather.4
  335.9 107.9 reduce-scatter.2
  449.7 135.0 reduce-scatter.4

commit v2 on v1

--- a/solution.py
+++ b/solution.py
@@ -1,6 +1,8 @@
 import jax
 import jax.numpy as jnp
 from jax import lax
+from jax.experimental import pallas as pl
+from jax.experimental.pallas import tpu as pltpu
 from jax.sharding import PartitionSpec as P
 
 D = 768
@@ -60,60 +62,154 @@
     )
 
 
-def split_heads(block):
-    return block.reshape(block.shape[0], H, HD)
-
-
-def row_scores(query, key_rows, segment):
-    scores = jnp.einsum(
-        "qhe,khe->hqk",
-        split_heads(query),
-        split_heads(key_rows),
-        preferred_element_type=jnp.float32,
-    ) * HD ** (-0.5)
-    same = segment[:, None] == segment[None, :]
-    return jnp.where(same[None], scores, masked_score)
-
-
-def attend_forward(pieces):
-    query, key_rows, value_rows, segment = pieces
-    scores = row_scores(query, key_rows, segment)
-    top = jnp.max(scores, axis=-1, keepdims=True)
-    exponent = jnp.exp(scores - top)
-    total = jnp.sum(exponent, axis=-1, keepdims=True)
-    attention = (exponent / total).astype(jnp.bfloat16)
-    context = jnp.einsum(
-        "hqk,khe->qhe", attention, split_heads(value_rows), preferred_element_type=jnp.float32
-    )
-    return (context.reshape(query.shape).astype(jnp.bfloat16), (top + jnp.log(total))[..., 0])
-
-
-def attend_backward(pieces):
-    query, key_rows, value_rows, segment, logsum, context_grad = pieces
-    scores = row_scores(query, key_rows, segment)
-    attention = jnp.exp(scores - logsum[..., None])
-    attention_low = attention.astype(jnp.bfloat16)
-    grad_heads = split_heads(context_grad)
-    value_grad = jnp.einsum(
-        "hqk,qhe->khe", attention_low, grad_heads, preferred_element_type=jnp.float32
-    )
-    attention_grad = jnp.einsum(
-        "qhe,khe->hqk", grad_heads, split_heads(value_rows), preferred_element_type=jnp.float32
-    )
-    inner_sum = jnp.sum(attention * attention_grad, axis=-1, keepdims=True)
-    score_grad = (attention * (attention_grad - inner_sum)).astype(jnp.bfloat16)
-    query_grad = jnp.einsum(
-        "hqk,khe->qhe", score_grad, split_heads(key_rows), preferred_element_type=jnp.float32
-    ) * HD ** (-0.5)
-    key_grad = jnp.einsum(
-        "hqk,qhe->khe", score_grad, split_heads(query), preferred_element_type=jnp.float32
-    ) * HD ** (-0.5)
-    shape = query.shape
-    return (
-        query_grad.reshape(shape).astype(jnp.bfloat16),
-        key_grad.reshape(shape).astype(jnp.bfloat16),
-        value_grad.reshape(shape).astype(jnp.bfloat16),
-    )
+def contract(left, right, left_axis, right_axis):
+    return lax.dot_general(
+        left, right, (((left_axis,), (right_axis,)), ((), ())), preferred_element_type=jnp.float32
+    )
+
+
+def own_lanes(block, half):
+    lane = lax.broadcasted_iota(jnp.int32, block.shape, 1)
+    return jnp.where((lane >= HD) == bool(half), block, jnp.zeros_like(block))
+
+
+def fill_mask(pair, column_ref, row_ref, mask_ref):
+    @pl.when(pair == 0)
+    def _():
+        same = column_ref[...] == row_ref[...]
+        mask_ref[...] = jnp.where(same, 0.0, masked_score)
+
+
+def forward_kernel(query_ref, key_ref, value_ref, column_ref, row_ref, out_ref, log_ref, mask_ref):
+    fill_mask(pl.program_id(1), column_ref, row_ref, mask_ref)
+    key_rows, value_rows = key_ref[...], value_ref[...]
+    scaled = query_ref[...] * jnp.bfloat16(HD ** (-0.5))
+    halves = []
+    for half in range(2):
+        scores = contract(key_rows, own_lanes(scaled, half), 1, 1) + mask_ref[...]
+        top = jnp.max(scores, axis=0, keepdims=True)
+        exponent = jnp.exp(scores - top)
+        total = jnp.sum(exponent, axis=0, keepdims=True)
+        attention = (exponent * (1.0 / total)).astype(jnp.bfloat16)
+        halves.append(contract(value_rows, attention, 0, 0)[half * HD : (half + 1) * HD])
+        log_ref[half : half + 1, :] = top + jnp.log(total)
+    out_ref[...] = jnp.concatenate(halves, axis=0).T.astype(jnp.bfloat16)
+
+
+def backward_kernel(
+    query_ref,
+    key_ref,
+    value_ref,
+    grad_ref,
+    column_ref,
+    row_ref,
+    log_ref,
+    query_out,
+    key_out,
+    value_out,
+    mask_ref,
+):
+    fill_mask(pl.program_id(1), column_ref, row_ref, mask_ref)
+    key_rows, value_rows, grad = key_ref[...], value_ref[...], grad_ref[...]
+    scaled = query_ref[...] * jnp.bfloat16(HD ** (-0.5))
+    query_halves, key_total, value_total = [], None, None
+    for half in range(2):
+        scaled_own, grad_own = own_lanes(scaled, half), own_lanes(grad, half)
+        scores = contract(key_rows, scaled_own, 1, 1) + mask_ref[...]
+        attention = jnp.exp(scores - log_ref[half : half + 1, :])
+        value_grad = contract(attention.astype(jnp.bfloat16), grad_own, 1, 0)
+        attention_grad = contract(value_rows, grad_own, 1, 1)
+        inner_sum = jnp.sum(attention * attention_grad, axis=0, keepdims=True)
+        score_grad = (attention * (attention_grad - inner_sum)).astype(jnp.bfloat16)
+        key_grad = contract(score_grad, scaled_own, 1, 0)
+        query_halves.append(contract(key_rows, score_grad, 0, 0)[half * HD : (half + 1) * HD])
+        key_total = key_grad if half == 0 else key_total + key_grad
+        value_total = value_grad if half == 0 else value_total + value_grad
+    query_grad = jnp.concatenate(query_halves, axis=0) * HD ** (-0.5)
+    query_out[...] = query_grad.T.astype(jnp.bfloat16)
+    key_out[...] = key_total.astype(jnp.bfloat16)
+    value_out[...] = value_total.astype(jnp.bfloat16)
+
+
+def attention_specs(rows, length):
+    pairs = H // 2
+    block = pl.BlockSpec((length, 2 * HD), lambda r, p: (r, p))
+    column = pl.BlockSpec((None, length, 1), lambda r, p: (r, 0, 0))
+    row = pl.BlockSpec((None, 1, length), lambda r, p: (r, 0, 0))
+    logs = pl.BlockSpec((None, None, 2, length), lambda r, p: (r, p, 0, 0))
+    options = dict(
+        grid=(rows, pairs),
+        scratch_shapes=[pltpu.VMEM((length, length), jnp.float32)],
+        compiler_params=pltpu.CompilerParams(dimension_semantics=("arbitrary", "arbitrary")),
+    )
+    return block, column, row, logs, options
+
+
+def attend_forward(query, key_rows, value_rows, segments):
+    rows, length = segments.shape
+    block, column, row, logs, options = attention_specs(rows, length)
+    return pl.pallas_call(
+        forward_kernel,
+        name="attend_forward",
+        in_specs=[block, block, block, column, row],
+        out_specs=[block, logs],
+        out_shape=[
+            jax.ShapeDtypeStruct(query.shape, jnp.bfloat16),
+            jax.ShapeDtypeStruct((rows, H // 2, 2, length), jnp.float32),
+        ],
+        cost_estimate=pl.CostEstimate(
+            flops=8 * rows * H * length * length * HD,
+            bytes_accessed=8 * rows * length * D,
+            transcendentals=rows * H * length * length,
+        ),
+        **options,
+    )(query, key_rows, value_rows, segments[:, :, None], segments[:, None, :])
+
+
+def attend_backward(query, key_rows, value_rows, grad, segments, logsum):
+    rows, length = segments.shape
+    block, column, row, logs, options = attention_specs(rows, length)
+    return pl.pallas_call(
+        backward_kernel,
+        name="attend_backward",
+        in_specs=[block, block, block, block, column, row, logs],
+        out_specs=[block, block, block],
+        out_shape=[jax.ShapeDtypeStruct(query.shape, jnp.bfloat16)] * 3,
+        cost_estimate=pl.CostEstimate(
+            flops=20 * rows * H * length * length * HD,
+            bytes_accessed=14 * rows * length * D,
+            transcendentals=rows * H * length * length,
+        ),
+        **options,
+    )(query, key_rows, value_rows, grad, segments[:, :, None], segments[:, None, :], logsum)
+
+
+def partners(devices, bit):
+    return [(i, i ^ (1 << bit)) for i in range(devices)]
+
+
+def gather_blocks(block, devices):
+    me = lax.axis_index("fsdp")
+    held = block[None]
+    for bit in reversed(range(devices.bit_length() - 1)):
+        other = lax.ppermute(held, "fsdp", partners(devices, bit))
+        upper = ((me >> bit) & 1) == 1
+        held = jnp.stack(
+            (jnp.where(upper, other, held), jnp.where(upper, held, other)), axis=1
+        ).reshape((-1,) + block.shape)
+    return held
+
+
+def scatter_blocks(terms, devices):
+    me = lax.axis_index("fsdp")
+    for bit in range(devices.bit_length() - 1):
+        pairs = terms.reshape((-1, 2) + terms.shape[1:])
+        upper = ((me >> bit) & 1) == 1
+        keep = jnp.where(upper, pairs[:, 1], pairs[:, 0])
+        send = jnp.where(upper, pairs[:, 0], pairs[:, 1])
+        other = lax.ppermute(send, "fsdp", partners(devices, bit))
+        terms = (keep.astype(jnp.float32) + other.astype(jnp.float32)).astype(jnp.bfloat16)
+    return terms[0]
 
 
 def per_device(
@@ -174,7 +270,7 @@
             inner_local[:, 3 * D :],
         )
     )
-    head_full = lax.all_gather(head, "fsdp", axis=0, tiled=True).reshape(devices, -1, D)
+    head_full = gather_blocks(head, devices)
     tail_full = lax.all_gather(tail, "fsdp", axis=0, tiled=True).reshape(devices, -1, D)
 
     def weight(full, start, size):
@@ -195,17 +291,11 @@
     )
     b_inner = small_full[:, 8 * piece :].reshape(FF)
 
-    def shaped(block):
-        return block.reshape(rows, length, D)
-
     flat = inputs.reshape(count, D)
     query = (matmul(flat, w_query) + b_query).astype(jnp.bfloat16)
     key_rows = matmul(flat, w_key).astype(jnp.bfloat16)
     value_rows = (matmul(flat, w_value) + b_value).astype(jnp.bfloat16)
-    context, logsum = lax.map(
-        attend_forward, (shaped(query), shaped(key_rows), shaped(value_rows), segments)
-    )
-    context = context.reshape(count, D)
+    context, logsum = attend_forward(query, key_rows, value_rows, segments)
     attended = matmul(context, w_output) + b_output
     first, normed_one, inv_one = norm_forward(
         flat.astype(jnp.float32) + attended, gain_one, shift_one
@@ -231,12 +321,6 @@
     def terms(grad):
         return grad.astype(jnp.bfloat16).reshape(devices, -1, D)
 
-    ffn_terms = jnp.concatenate(
-        [terms(outer_weight_grad)] + [terms(block) for block in inner_weight_grads], axis=1
-    )
-    ffn_sum = lax.psum_scatter(
-        ffn_terms.reshape(-1, D), "fsdp", scatter_dimension=0, tiled=True
-    ).astype(jnp.float32)
     first_grad = second_grad + matmul_right_t(inner_grad, w_inner)
     attn_pre_grad, attn_gain_grad, attn_shift_grad = norm_backward(
         first_grad, normed_one, inv_one, gain_one
@@ -245,20 +329,19 @@
     output_bias_grad = jnp.sum(attended_grad.astype(jnp.float32), axis=0)
     output_weight_grad = matmul_left_t(context, attended_grad)
     context_grad = matmul_right_t(attended_grad, w_output).astype(jnp.bfloat16)
-    query_grad, key_grad, value_grad = lax.map(
-        attend_backward,
-        (
-            shaped(query),
-            shaped(key_rows),
-            shaped(value_rows),
-            segments,
-            logsum,
-            shaped(context_grad),
-        ),
-    )
-    query_grad = query_grad.reshape(count, D)
-    key_grad = key_grad.reshape(count, D)
-    value_grad = value_grad.reshape(count, D)
+    early_terms = jnp.concatenate(
+        [terms(outer_weight_grad)]
+        + [terms(block) for block in inner_weight_grads]
+        + [terms(output_weight_grad)],
+        axis=1,
+    ).reshape(-1, D)
+    early_terms, context_grad = lax.optimization_barrier((early_terms, context_grad))
+    ffn_sum = lax.psum_scatter(
+        early_terms, "fsdp", scatter_dimension=0, tiled=True
+    ).astype(jnp.float32)
+    query_grad, key_grad, value_grad = attend_backward(
+        query, key_rows, value_rows, context_grad, segments, logsum
+    )
     query_weight_grad = matmul_left_t(flat, query_grad)
     key_weight_grad = matmul_left_t(flat, key_grad)
     value_weight_grad = matmul_left_t(flat, value_grad)
@@ -288,7 +371,6 @@
     )
     attn_terms = jnp.concatenate(
         (
-            terms(output_weight_grad),
             terms(query_weight_grad),
             terms(key_weight_grad),
             terms(value_weight_grad),
@@ -296,9 +378,7 @@
         ),
         axis=1,
     )
-    attn_sum = lax.psum_scatter(
-        attn_terms.reshape(-1, D), "fsdp", scatter_dimension=0, tiled=True
-    ).astype(jnp.float32)
+    attn_sum = scatter_blocks(attn_terms, devices).astype(jnp.float32)
     input_grad = (
         attn_pre_grad
         + matmul_right_t(query_grad, w_query)
@@ -309,7 +389,7 @@
     def owned(total, start, size):
         return total[start : start + size].reshape(-1)
 
-    small_sum = attn_sum[4 * piece, : (8 + share) * piece]
+    small_sum = attn_sum[3 * piece, : (8 + share) * piece]
 
     def vector(i, size=1):
         return small_sum[i * piece : (i + size) * piece]
@@ -320,12 +400,12 @@
     return (
         result.reshape(rows, length, D).astype(jnp.bfloat16),
         input_grad.reshape(rows, length, D).astype(jnp.bfloat16),
+        owned(attn_sum, 0, piece),
+        vector(0),
         owned(attn_sum, piece, piece),
-        vector(0),
         owned(attn_sum, 2 * piece, piece),
-        owned(attn_sum, 3 * piece, piece),
         vector(1),
-        owned(attn_sum, 0, piece),
+        owned(ffn_sum, 2 * share * piece, piece),
         vector(2),
         vector(3),
         vector(4),

time: 602 us -> 394 us (0.65)
  waiting for transfers between devices: 311 us -> 163 us
  matrix products: 148 us -> 76.6 us
  Pallas kernels: 0 us -> 51 us
  local copies, waits for them, and re-layouts: 84.4 us -> 43.7 us
  starting transfers between devices: 0.16 us -> 22.5 us
  other arithmetic: 36.4 us -> 15.8 us
    reduce_scatter x2 -> x1, waiting for transfers between devices: 206 us -> 34.2 us  [per_device(): lax.psum_scatter(early_terms, 'fsdp', scatter_dimension=0, tiled=True)]
    ppermute x0 -> x10, waiting for transfers between devices: none -> 128 us  [the longest x5 68.8 us: gather_blocks(): other = lax.ppermute(held, 'fsdp', partners(devices, bit))]
    all_gather x1 -> x0, waiting for transfers between devices: 58.9 us -> none  [per_device(): lax.all_gather(head, 'fsdp', axis=0, tiled=True).reshape(devices, -1, D)]
    dot_general x14 -> x0, matrix products: 58.5 us -> none  [the longest x2 21.9 us: attend_backward(): jnp.einsum('qhe,khe->hqk', grad_heads, split_heads(value_rows), preferred...]
    pallas_call x0 -> x2, Pallas kernels: none -> 51 us  [the longest x1 31.9 us: attend_backward(): pl.pallas_call(backward_kernel, name='attend_backward', in_specs=[block,...]
    all_gather x1, waiting for transfers between devices: 45.8 us -> 0.01 us  [per_device(): lax.all_gather(tail, 'fsdp', axis=0, tiled=True).reshape(devices, -1, D)]
    ppermute x0 -> x10, starting transfers between devices: none -> 22.4 us  [the longest x5 12.2 us: scatter_blocks(): other = lax.ppermute(send, 'fsdp', partners(devices, bit))]
    convert_element_type x3 -> x4, other arithmetic: 14.8 us -> 1.27 us  [the longest x3 1.23 us: scatter_blocks(): (keep.astype(jnp.float32) + other.astype(jnp.float32)).astype(jnp.bfloat16)]
  transfers between devices with their start and end apart: 4 -> 12, of which waited for: 4 -> 11; matrix products, arithmetic and copies ran while one was open for 15% -> 12% of each run, Pallas kernels for 0% -> 13%
where the time goes in v2:
time: 394 us; the launch traced here: 387 us
  waiting for transfers between devices  163 us (41%)
  matrix products  76.6 us (19%)
  Pallas kernels  51 us (13%)
  local copies, waits for them, and re-layouts  43.7 us (11%)
  starting transfers between devices  22.5 us (6%)
  other arithmetic  15.8 us (4%)
  between operations  15.3 us (4%)
    ppermute x5, waiting for transfers between devices, gather_blocks(): other = lax.ppermute(held, 'fsdp', partners(devices, bit))  68.8 us
    ppermute x5, waiting for transfers between devices, scatter_blocks(): other = lax.ppermute(send, 'fsdp', partners(devices, bit))  59.5 us
    reduce_scatter x1, waiting for transfers between devices, per_device(): lax.psum_scatter(early_terms, 'fsdp', scatter_dimension=0, tiled=True)  34.2 us
    pallas_call x1, Pallas kernels, attend_backward(): pl.pallas_call(backward_kernel, name='attend_backward', in_specs=[block,...  31.9 us
    dot_general x6, matrix products, matmul_right_t(): lax.dot_general(left, right, (((1,), (1,)), ((), ())), preferred_element_...  30.2 us
    dot_general x6, matrix products, matmul(): return jnp.dot(left, right, preferred_element_type=jnp.float32)  25.6 us
    dot_general x9, matrix products, matmul_left_t(): lax.dot_general(left, right, (((0,), (0,)), ((), ())), preferred_element_...  20.8 us
    pallas_call x1, Pallas kernels, attend_forward(): pl.pallas_call(forward_kernel, name='attend_forward', in_specs=[block, bl...  19.1 us
  transfers between devices with their start and end apart: 12, of which 11 were waited for; matrix products, arithmetic and copies ran while one was open for 12% of the time, Pallas kernels for 13%

profile of v2, /device:TPU:0, one launch (start us, length us, event | category | flops | bytes accessed | tf_op | source)
XLA Modules:
  0.0 387.4 jit_solution(13178562408540602401)
XLA Ops:
  7.2 1.0 reshape.412
  9.1 1.1 reshape.411
  13.5 6.1 %concatenate.47 = bf16[288]{0:T(512)(128)(2,1)S(1)} concatenate(bf16[24]{0:T(256)(128)(2,1)} %param.21, bf16[24]{0:T(256)(128)(2,1)} %param.24, bf16[24]{0:T(256)(128)(2,1)} %param.26, bf16[24]{0:T(256)(128)(2,1)} %param.27, bf16[24]{0:T(256)(128)(2,1)} %param.28, bf16[24]{0:T(256)(128)(2,1)} %param.32, bf16[24]{0:T(256)(128)(2,1)} %param.33, bf16[24]{0:T(256)(128)(2,1)} %param.34, ...), dimensions={0} | concatenate | bytes 1152 | tf_op jit(solution)/shard_map/concatenate | solution.py:240
  19.6 4.1 %collective-permute-start = (bf16[1,80,768]{2,1,0:T(8,128)(2,1)S(1)}, bf16[1,80,768]{2,1,0:T(8,128)(2,1)S(1)}, u32[]{:S(2)}, u32[]{:S(2)}) collective-permute-start(bf16[1,80,768]{2,1,0:T(8,128)(2,1)S(1)} %fusion.58), channel_id=1, source_target_pairs={{0,16},{1,17},{2,18},{3,19},{4,20},{5,21},{6,22},{7,23},{8,24},{9,... | collective-permute-start | bytes 368648 | tf_op jit(solution)/shard_map/ppermute | solution.py:195
  23.7 10.2 %collective-permute-done = bf16[1,80,768]{2,1,0:T(8,128)(2,1)S(1)} collective-permute-done((bf16[1,80,768]{2,1,0:T(8,128)(2,1)S(1)}, bf16[1,80,768]{2,1,0:T(8,128)(2,1)S(1)}, u32[]{:S(2)}, u32[]{:S(2)}) %collective-permute-start) | collective-permute-done | bytes 122912 | tf_op jit(solution)/shard_map/ppermute | solution.py:195
  34.0 1.7 collective-permute-start.1
  35.7 6.4 %collective-permute-done.1 = bf16[2,80,768]{2,1,0:T(8,128)(2,1)S(1)} collective-permute-done((bf16[2,80,768]{2,1,0:T(8,128)(2,1)S(1)}, bf16[2,80,768]{2,1,0:T(8,128)(2,1)S(1)}, u32[]{:S(2)}, u32[]{:S(2)}) %collective-permute-start.1) | collective-permute-done | bytes 245792 | tf_op jit(solution)/shard_map/ppermute | solution.py:195
  42.3 2.1 collective-permute-start.2
  44.4 15.4 %collective-permute-done.2 = bf16[4,80,768]{2,1,0:T(8,128)(2,1)S(1)} collective-permute-done((bf16[4,80,768]{2,1,0:T(8,128)(2,1)S(1)}, bf16[4,80,768]{2,1,0:T(8,128)(2,1)S(1)}, u32[]{:S(2)}, u32[]{:S(2)}) %collective-permute-start.2) | collective-permute-done | bytes 491552 | tf_op jit(solution)/shard_map/ppermute | solution.py:195
  60.0 2.1 collective-permute-start.3
  62.1 34.2 %collective-permute-done.3 = bf16[8,80,768]{2,1,0:T(8,128)(2,1)S(1)} collective-permute-done((bf16[8,80,768]{2,1,0:T(8,128)(2,1)S(1)}, bf16[8,80,768]{2,1,0:T(8,128)(2,1)S(1)}, u32[]{:S(2)}, u32[]{:S(2)}) %collective-permute-start.3) | collective-permute-done | bytes 983072 | tf_op jit(solution)/shard_map/ppermute | solution.py:195
  97.4 1.1 copy.106.column_ref
  98.4 2.6 collective-permute-done.4
  101.0 1.8 select_bitcast_fusion.2
  103.2 2.0 copy-done.1
  107.0 2.3 fusion.68
  109.4 2.6 fusion.36.key_ref
  112.1 2.5 fusion.38.value_ref
  114.6 2.5 fusion.37.query_ref
  117.2 19.1 %attend_forward.1 = (bf16[1024,768]{1,0:T(8,128)(2,1)}, f32[2,6,2,512]{3,2,1,0:T(2,128)}) custom-call(bf16[1024,768]{1,0:T(8,128)(2,1)} %fusion.37.query_ref, bf16[1024,768]{1,0:T(8,128)(2,1)} %fusion.36.key_ref, bf16[1024,768]{1,0:T(8,128)(2,1)} %fusion.38.value_ref, s32[2,512,1]{2,1,0:T(8,128)} %copy.106.column_ref, s32[2,1,512]{2,1,0:T(1,128)} %broadcast_in_dim.8.row_ref), custom_call_target="tpu_custom_call" | custom-call | flops 3221225472 | bytes 6291456 | tf_op jit(solution)/shard_map/attend_forward/pallas_call | solution.py:151
  136.3 3.1 fusion.67
  139.4 2.8 slice.311
  142.7 1.5 fusion.71
  145.4 10.8 %multiply_convert_fusion = (bf16[1024,3072]{1,0:T(8,128)(2,1)S(1)}, f32[1024,3072]{1,0:T(8,128)}) fusion(f32[3072]{0:T(1024)S(1)} %add.148, bf16[1024,768]{1,0:T(8,128)(2,1)S(1)} %fusion.14, bf16[768,768]{1,0:T(8,128)(2,1)S(1)} %bitcast.268, bf16[768,768]{1,0:T(8,128)(2,1)S(1)} %bitcast.270, bf16[768,768]{1,0:T(8,128)(2,1)S(1)} %bitcast.272, ...), kind=kOutput, calls=%fused_computation.7 | convolution fusion | flops 4869586944 | bytes 25178112 | tf_op jit(solution)/shard_map/dot_general | solution.py:21
  156.2 5.5 %fusion.72 = (f32[1024]{0:T(1024)S(1)}, f32[1024,768]{1,0:T(8,128)S(1)}) fusion(f32[768]{0:T(1024)S(1)} %add.152, bf16[1024,3072]{1,0:T(8,128)(2,1)S(1)} %get-tuple-element.86, bf16[3072,768]{1,0:T(8,128)(2,1)S(1)} %bitcast.253, f32[768]{0:T(1024)S(1)} %add.145, f32[768]{0:T(1024)S(1)} %mul.136, f32[1024]{0:T(1024)S(1)} %add_rsqrt_fusion.1, ...), kind=kOutput, calls=%fused_computation.178 | convolution fusion | flops 4837342208 | bytes 17323008 | tf_op jit(solution)/shard_map/dot_general | solution.py:21
  162.2 2.7 fusion.13
  164.9 1.2 convert_reduce_fusion.1
  166.1 13.2 %fusion.73 = (bf16[3072]{0:T(1024)(128)(2,1)S(1)}, bf16[1024,3072]{1,0:T(8,128)(2,1)}) fusion(f32[1024,3072]{1,0:T(8,128)} %get-tuple-element.87, f32[3072]{0:T(1024)S(1)} %add.148, bf16[3072,768]{1,0:T(8,128)(2,1)S(1)} %bitcast.254, f32[1024,768]{1,0:T(8,128)S(1)} %get-tuple-element.46), kind=kOutput, calls=%fused_computation.179 | convolution fusion | flops 4870370304 | bytes 26757120 | tf_op jit(solution)/shard_map/dot_general | solution.py:31
  179.3 8.9 %multiply_reduce_fusion = (bf16[768]{0:T(1024)(128)(2,1)S(1)}, f32[1024]{0:T(1024)S(1)}, f32[1024]{0:T(1024)S(1)}, bf16[768]{0:T(1024)(128)(2,1)S(1)}, f32[1024,768]{1,0:T(8,128)S(1)}) fusion(f32[1024,768]{1,0:T(8,128)S(1)} %get-tuple-element.85, f32[1024]{0:T(1024)S(1)} %add_rsqrt_fusion.1, f32[1024]{0:T(1024)S(1)} %broadcast_multiply_fusion.4, ...), kind=kOutput, calls=%fused_computation.24 | convolution fusion | flops 4858572800 | bytes 20469760 | tf_op jit(solution)/shard_map/dot_general | solution.py:31
  188.2 3.0 fusion.33
  191.5 1.5 fusion.30
  193.0 1.5 fusion.27
  194.5 1.5 fusion.24
  196.2 5.8 %convolution_convert_fusion = bf16[3072,768]{1,0:T(8,128)(2,1)S(1)} fusion(bf16[1024,3072]{1,0:T(8,128)(2,1)S(1)} %bitcast.303, f32[1024,768]{1,0:T(8,128)S(1)} %get-tuple-element.46), kind=kOutput, calls=%fused_computation.9 | convolution fusion | flops 4834983936 | bytes 14155776 | tf_op jit(solution)/shard_map/dot_general | solution.py:25
  202.1 1.1 convert_reduce_fusion
  203.5 1.5 convolution_convert_fusion.6
  205.0 2.6 convolution_convert_fusion.2.grad_ref
  207.6 2.6 constant_dynamic-update-slice_fusion.11
  210.2 1.1 constant_dynamic-update-slice_fusion.10
  211.3 1.2 constant_dynamic-update-slice_fusion.9
  212.5 1.1 constant_dynamic-update-slice_fusion.8
  213.6 1.1 constant_dynamic-update-slice_fusion.7
  214.7 1.1 constant_dynamic-update-slice_fusion.6
  216.2 31.9 %attend_backward.1 = (bf16[1024,768]{1,0:T(8,128)(2,1)}, bf16[1024,768]{1,0:T(8,128)(2,1)}, bf16[1024,768]{1,0:T(8,128)(2,1)}) custom-call(bf16[1024,768]{1,0:T(8,128)(2,1)} %fusion.37.query_ref, bf16[1024,768]{1,0:T(8,128)(2,1)} %fusion.36.key_ref, bf16[1024,768]{1,0:T(8,128)(2,1)} %fusion.38.value_ref, ...), custom_call_target="tpu_custom_call" | custom-call | flops 8053063680 | bytes 11010048 | tf_op jit(solution)/shard_map/attend_backward/pallas_call | solution.py:172
  248.1 1.9 reduce.2
  250.1 1.8 reduce.3
  253.1 3.1 convolution_convert_fusion.5
  256.3 1.5 convolution_convert_fusion.4
  257.9 1.5 convolution_convert_fusion.3
  260.4 3.8 collective-permute-done.5
  264.9 2.4 collective-permute-start.6
  267.3 31.6 %collective-permute-done.6 = bf16[8,80,768]{2,1,0:T(8,128)(2,1)S(1)} collective-permute-done((bf16[8,80,768]{2,1,0:T(8,128)(2,1)S(1)}, bf16[8,80,768]{2,1,0:T(8,128)(2,1)S(1)}, u32[]{:S(2)}, u32[]{:S(2)}) %collective-permute-start.6) | collective-permute-done | bytes 983072 | tf_op jit(solution)/shard_map/ppermute | solution.py:210
  299.3 0.9 collective-permute-start.7
  300.3 1.4 fusion.74
  301.7 18.6 %collective-permute-done.7 = bf16[4,80,768]{2,1,0:T(8,128)(2,1)S(1)} collective-permute-done((bf16[4,80,768]{2,1,0:T(8,128)(2,1)S(1)}, bf16[4,80,768]{2,1,0:T(8,128)(2,1)S(1)}, u32[]{:S(2)}, u32[]{:S(2)}) %collective-permute-start.7) | collective-permute-done | bytes 491552 | tf_op jit(solution)/shard_map/ppermute | solution.py:210
  320.5 1.8 collective-permute-start.8
  322.3 1.4 fusion.75
  323.7 3.1 collective-permute-done.8
  326.9 6.8 %collective-permute-start.9 = (bf16[1,80,768]{2,1,0:T(8,128)(2,1)S(1)}, bf16[1,80,768]{2,1,0:T(8,128)(2,1)S(1)}, u32[]{:S(2)}, u32[]{:S(2)}) collective-permute-start(bf16[1,80,768]{2,1,0:T(8,128)(2,1)S(1)} %select_bitcast_fusion.9), channel_id=1, source_target_pairs={{0,16},{1,17},{2,18},{3,19},{4,20},{5,21},{6,22},{7,23},{8,24},{9,... | collective-permute-start | bytes 368648 | tf_op jit(solution)/shard_map/ppermute | solution.py:210
  333.7 2.6 add_convert_fusion
  336.3 2.5 collective-permute-done.9
  342.0 34.2 %reduce-scatter.2.cloned.1.call-done = bf16[216,768]{1,0:T(8,128)(2,1)} async-done(((bf16[6912,768]{1,0:T(8,128)(2,1)}), bf16[216,768]{1,0:T(8,128)(2,1)}) %reduce-scatter.2.cloned.1.call-update) | async-done | bytes 331792 | tf_op jit(solution)/shard_map/reduce_scatter | solution.py:339
  376.2 0.9 fusion.69
  377.9 0.9 slice.343
  (146 shorter events, 20.1 us)
Async XLA Ops:
  7.2 129.1 %all-gather.2.cloned.1.call-start = ((), (), s32[]{:S(2)}) async-start(), calls=%async_computation.1 | async-start | bytes 10948608 | tf_op jit(solution)/shard_map/all_gather | solution.py:274
  10.2 0.7 copy-start.10
  10.9 365.3 %reduce-scatter.2.cloned.1.call-start = ((), (), s32[]{:S(2)}) async-start(), calls=%async_computation.2 | async-start | bytes 10948608 | tf_op jit(solution)/shard_map/reduce_scatter | solution.py:339
  19.6 14.3 %collective-permute-start = (bf16[1,80,768]{2,1,0:T(8,128)(2,1)S(1)}, bf16[1,80,768]{2,1,0:T(8,128)(2,1)S(1)}, u32[]{:S(2)}, u32[]{:S(2)}) collective-permute-start(bf16[1,80,768]{2,1,0:T(8,128)(2,1)S(1)} %fusion.58), channel_id=1, source_target_pairs={{0,16},{1,17},{2,18},{3,19},{4,20},{5,21},{6,22},{7,23},{8,24},{9,... | collective-permute-start | bytes 368648 | tf_op jit(solution)/shard_map/ppermute | solution.py:195
  34.0 8.1 %collective-permute-start.1 = (bf16[2,80,768]{2,1,0:T(8,128)(2,1)S(1)}, bf16[2,80,768]{2,1,0:T(8,128)(2,1)S(1)}, u32[]{:S(2)}, u32[]{:S(2)}) collective-permute-start(bf16[2,80,768]{2,1,0:T(8,128)(2,1)S(1)} %maximum_bitcast_fusion.1), channel_id=1, source_target_pairs={{0,8},{1,9},{2,10},{3,11},{4,12},{5,13},{6,14},{7,15},{8,0},{9,1},... | collective-permute-start | bytes 737288 | tf_op jit(solution)/shard_map/ppermute | solution.py:195
  42.3 17.5 %collective-permute-start.2 = (bf16[4,80,768]{2,1,0:T(8,128)(2,1)S(1)}, bf16[4,80,768]{2,1,0:T(8,128)(2,1)S(1)}, u32[]{:S(2)}, u32[]{:S(2)}) collective-permute-start(bf16[4,80,768]{2,1,0:T(8,128)(2,1)S(1)} %bitcast.261), channel_id=1, source_target_pairs={{0,4},{1,5},{2,6},{3,7},{4,0},{5,1},{6,2},{7,3},{8,12},{9,13},{10,... | collective-permute-start | bytes 1474568 | tf_op jit(solution)/shard_map/ppermute | solution.py:195
  60.0 36.3 %collective-permute-start.3 = (bf16[8,80,768]{2,1,0:T(8,128)(2,1)S(1)}, bf16[8,80,768]{2,1,0:T(8,128)(2,1)S(1)}, u32[]{:S(2)}, u32[]{:S(2)}) collective-permute-start(bf16[8,80,768]{2,1,0:T(8,128)(2,1)S(1)} %bitcast.260), channel_id=1, source_target_pairs={{0,2},{1,3},{2,0},{3,1},{4,6},{5,7},{6,4},{7,5},{8,10},{9,11},{10,... | collective-permute-start | bytes 2949128 | tf_op jit(solution)/shard_map/ppermute | solution.py:195
  62.1 34.7 %copy-start.11 = (s32[2,512]{1,0:T(2,128)S(1)}, s32[2,512]{1,0:T(2,128)}, u32[]{:S(2)}) copy-start(s32[2,512]{1,0:T(2,128)} %param.19) | copy-start | bytes 12292
  96.7 4.3 %collective-permute-start.4 = (bf16[16,80,768]{2,1,0:T(8,128)(2,1)S(1)}, bf16[16,80,768]{2,1,0:T(8,128)(2,1)}, u32[]{:S(2)}, u32[]{:S(2)}) collective-permute-start(bf16[16,80,768]{2,1,0:T(8,128)(2,1)S(1)} %bitcast.252), channel_id=1, source_target_pairs={{0,1},{1,0},{2,3},{3,2},{4,5},{5,4},{6,7},{7,6},{8,9},{9,8},{10,11... | collective-permute-start | bytes 5898248 | tf_op jit(solution)/shard_map/ppermute | solution.py:195
  102.8 3.7 copy-start
  103.2 2.0 copy-start.1
  107.0 2.5 copy-start.12
  109.3 2.8 copy-start.8
  109.3 2.8 copy-start.5
  139.4 2.8 copy-start.13
  139.4 3.3 copy-start.17
  156.2 5.5 %copy-start.19 = (bf16[1024,3072]{1,0:T(8,128)(2,1)}, bf16[1024,3072]{1,0:T(8,128)(2,1)S(1)}, u32[]{:S(2)}) copy-start(bf16[1024,3072]{1,0:T(8,128)(2,1)S(1)} %get-tuple-element.86) | copy-start | bytes 18874372
  188.2 3.3 copy-start.15
  193.0 3.0 slice-start
  194.5 1.8 slice-start.1
  202.1 1.4 copy-start.18
  203.2 1.7 copy-start.2
  248.1 4.9 %copy-start.7 = (bf16[1024,768]{1,0:T(8,128)(2,1)S(1)}, bf16[1024,768]{1,0:T(8,128)(2,1)}, u32[]{:S(2)}) copy-start(bf16[1024,768]{1,0:T(8,128)(2,1)} %get-tuple-element.27) | copy-start | bytes 4718596
  253.1 3.2 copy-start.14
  253.1 3.2 copy-start.16
  256.3 1.6 copy-start.4
  260.0 4.2 %collective-permute-start.5 = (bf16[16,80,768]{2,1,0:T(8,128)(2,1)S(1)}, bf16[16,80,768]{2,1,0:T(8,128)(2,1)S(1)}, u32[]{:S(2)}, u32[]{:S(2)}) collective-permute-start(bf16[16,80,768]{2,1,0:T(8,128)(2,1)S(1)} %select_bitcast_fusion), channel_id=1, source_target_pairs={{0,1},{1,0},{2,3},{3,2},{4,5},{5,4},{6,7},{7,6},{8,9},{9,8},{10,11... | collective-permute-start | bytes 5898248 | tf_op jit(solution)/shard_map/ppermute | solution.py:210
  264.9 34.0 %collective-permute-start.6 = (bf16[8,80,768]{2,1,0:T(8,128)(2,1)S(1)}, bf16[8,80,768]{2,1,0:T(8,128)(2,1)S(1)}, u32[]{:S(2)}, u32[]{:S(2)}) collective-permute-start(bf16[8,80,768]{2,1,0:T(8,128)(2,1)S(1)} %fusion.39), channel_id=1, source_target_pairs={{0,2},{1,3},{2,0},{3,1},{4,6},{5,7},{6,4},{7,5},{8,10},{9,11},{10,... | collective-permute-start | bytes 2949128 | tf_op jit(solution)/shard_map/ppermute | solution.py:210
  299.3 23.0 %copy-start.9 = (bf16[32,24,768]{2,1,0:T(8,128)(2,1)S(1)}, bf16[32,24,768]{2,1,0:T(8,128)(2,1)}, u32[]{:S(2)}) copy-start(bf16[32,24,768]{2,1,0:T(8,128)(2,1)} %copy-done.8) | copy-start | bytes 3538948
  299.3 21.0 %collective-permute-start.7 = (bf16[4,80,768]{2,1,0:T(8,128)(2,1)S(1)}, bf16[4,80,768]{2,1,0:T(8,128)(2,1)S(1)}, u32[]{:S(2)}, u32[]{:S(2)}) collective-permute-start(bf16[4,80,768]{2,1,0:T(8,128)(2,1)S(1)} %fusion.48), channel_id=1, source_target_pairs={{0,4},{1,5},{2,6},{3,7},{4,0},{5,1},{6,2},{7,3},{8,12},{9,13},{10,... | collective-permute-start | bytes 1474568 | tf_op jit(solution)/shard_map/ppermute | solution.py:210
  320.5 13.2 %copy-start.6 = (bf16[32,24,768]{2,1,0:T(8,128)(2,1)S(1)}, bf16[32,24,768]{2,1,0:T(8,128)(2,1)}, u32[]{:S(2)}) copy-start(bf16[32,24,768]{2,1,0:T(8,128)(2,1)} %copy-done.5) | copy-start | bytes 3538948
  320.5 6.3 %collective-permute-start.8 = (bf16[2,80,768]{2,1,0:T(8,128)(2,1)S(1)}, bf16[2,80,768]{2,1,0:T(8,128)(2,1)S(1)}, u32[]{:S(2)}, u32[]{:S(2)}) collective-permute-start(bf16[2,80,768]{2,1,0:T(8,128)(2,1)S(1)} %fusion.52), channel_id=1, source_target_pairs={{0,8},{1,9},{2,10},{3,11},{4,12},{5,13},{6,14},{7,15},{8,0},{9,1},... | collective-permute-start | bytes 737288 | tf_op jit(solution)/shard_map/ppermute | solution.py:210
  322.3 11.4 %copy-start.3 = (f32[1024,768]{1,0:T(8,128)S(1)}, f32[1024,768]{1,0:T(8,128)}, u32[]{:S(2)}) copy-start(f32[1024,768]{1,0:T(8,128)} %copy-done.2) | copy-start | bytes 9437188
  326.9 11.9 %collective-permute-start.9 = (bf16[1,80,768]{2,1,0:T(8,128)(2,1)S(1)}, bf16[1,80,768]{2,1,0:T(8,128)(2,1)S(1)}, u32[]{:S(2)}, u32[]{:S(2)}) collective-permute-start(bf16[1,80,768]{2,1,0:T(8,128)(2,1)S(1)} %select_bitcast_fusion.9), channel_id=1, source_target_pairs={{0,16},{1,17},{2,18},{3,19},{4,20},{5,21},{6,22},{7,23},{8,24},{9,... | collective-permute-start | bytes 368648 | tf_op jit(solution)/shard_map/ppermute | solution.py:210
Sparse Core Ops, SparseCore 0:
  11.5 106.7 all-gather.1
  215.9 160.2 reduce-scatter.1
